TPU v7x, 32 devices: a whole 2x2x4 slice. The times are simulated.
32 devices in a mesh: orb: 16 (over z, y, core), fft: 2 (over x).
Axes of the slice: x: 2, y: 2, z: 4, core: 2. Of those that a mesh axis runs over, the one named last changes fastest.
Arguments:
- orbitals: bfloat16 [128, 256, 256], P('orb', 'fft'), may hold values from -6 to 6
- kernel: float32 [256, 256], P('fft'), may hold values from 0.02 to 2
- partner_owner: int32 [128, 2, 1], P('orb'), may hold values from 0 to 15; in each aligned block of 16 rows (0 to 15, 16 to 31, ..., all dimensions but the last counted through in order) at most 2 rows name the same one
- partner_local: int32 [128, 2], P('orb'), may hold values from 0 to 7
Outputs:
- exchange_term: float32 [128, 256, 256], P('orb', 'fft')
Inputs may be any that keep to these rules, and one draw needn't show every extreme that they name: `partner_owner`: among the 16 partners named on one index of orb, no owner is named more than 2 times, a bound that some block reaches; every owner is named somewhere.
All inputs are finite; a program needn't handle non-finite values.
Results may differ from a plain program's by a relative error of at most 0.0004.
Values may be sent and summed in bfloat16 or wider, within the bound.
A program may use at most 64 MiB of HBM per device.

v0:
```python
import math

import jax
import jax.numpy as jnp
from jax import lax
from jax.sharding import PartitionSpec as P


def tables(length):
    series = jnp.arange(length, dtype=jnp.int32)
    phase = series[:, None] * series[None, :] % length
    angle = phase.astype(jnp.float32) * (2.0 * math.pi / length)
    return (jnp.cos(angle), jnp.sin(angle))


def product(form, left, right):
    return jnp.einsum(form, left, right, precision=lax.Precision.HIGHEST)


def group_potential(density, kernel):
    grouped = lax.all_to_all(density, "fft", split_axis=0, concat_axis=1, tiled=True)
    whole = lax.all_gather(kernel, "fft", axis=0, tiled=True)
    full_x = grouped.shape[1]
    width_y = grouped.shape[2]
    cos_y, sin_y = tables(width_y)
    cos_x, sin_x = tables(full_x)
    real_y = product("txy,yk->txk", grouped, cos_y)
    imag_y = -product("txy,yk->txk", grouped, sin_y)
    f_real = product("txk,xq->tqk", real_y, cos_x) + product("txk,xq->tqk", imag_y, sin_x)
    f_imag = product("txk,xq->tqk", imag_y, cos_x) - product("txk,xq->tqk", real_y, sin_x)
    weight = whole.T
    g_real = weight[None] * f_real
    g_imag = weight[None] * f_imag
    h_real = product("tqk,qx->txk", g_real, cos_x) - product("tqk,qx->txk", g_imag, sin_x)
    h_imag = product("tqk,qx->txk", g_real, sin_x) + product("tqk,qx->txk", g_imag, cos_x)
    spread = product("txk,ky->txy", h_real, cos_y) - product("txk,ky->txy", h_imag, sin_y)
    spread = spread / (full_x * width_y)
    return lax.all_to_all(spread, "fft", split_axis=1, concat_axis=0, tiled=True)


def on_device(orbitals, kernel, partner_owner, partner_local):
    peer_count = lax.axis_size("orb")
    orb_dev, rows_x, width_y = orbitals.shape
    task_count = partner_local.shape[0]
    wanted_count = 2 * task_count
    capacity = max(2, (4 * task_count + peer_count - 1) // peer_count)
    owner_ids = partner_owner.reshape(wanted_count)
    local_ids = partner_local.reshape(wanted_count)
    peer_ids = jnp.arange(peer_count, dtype=jnp.int32)
    owner_hot = (owner_ids[:, None] == peer_ids[None, :]).astype(jnp.int32)
    earlier = jnp.cumsum(owner_hot, axis=0) - owner_hot
    position = jnp.sum(earlier * owner_hot, axis=1)
    target = owner_ids * capacity + position
    slot_ids = jnp.arange(peer_count * capacity, dtype=jnp.int32)
    placed = target[:, None] == slot_ids[None, :]
    wanted = jnp.max(jnp.where(placed, local_ids[:, None], -1), axis=0).reshape(
        peer_count, capacity
    )
    asked = lax.all_to_all(wanted, "orb", split_axis=0, concat_axis=0, tiled=True)
    flat_asked = asked.reshape(peer_count * capacity)
    present = flat_asked >= 0
    picked = jnp.take(orbitals, jnp.clip(flat_asked, 0, orb_dev - 1), axis=0)
    served = jnp.where(present[:, None, None], picked, jnp.zeros_like(picked))
    served = served.reshape(peer_count, capacity, rows_x, width_y)
    arrived = lax.all_to_all(served, "orb", split_axis=0, concat_axis=0, tiled=True)
    arrived = arrived.reshape(peer_count * capacity, rows_x, width_y)
    chosen = (
        jnp.take(arrived, target, axis=0)
        .reshape(task_count, 2, rows_x, width_y)
        .astype(jnp.float32)
    )
    left_orbital = chosen[:, 0]
    right_orbital = chosen[:, 1]
    density = left_orbital * right_orbital
    potential = group_potential(density, kernel)
    contrib = jnp.stack([potential * right_orbital, potential * left_orbital], axis=1)
    contrib = contrib.reshape(wanted_count, rows_x, width_y)
    outgoing = (
        jnp.zeros((peer_count * capacity, rows_x, width_y), jnp.float32).at[target].set(contrib)
    )
    outgoing = outgoing.reshape(peer_count, capacity, rows_x, width_y)
    incoming = lax.all_to_all(outgoing, "orb", split_axis=0, concat_axis=0, tiled=True)
    incoming = incoming.reshape(peer_count * capacity, rows_x * width_y)
    select = (flat_asked[None, :] == jnp.arange(orb_dev, dtype=jnp.int32)[:, None]).astype(
        jnp.float32
    )
    total = jnp.dot(select, incoming, precision=lax.Precision.HIGHEST)
    return (-total).reshape(orb_dev, rows_x, width_y)


def solution(mesh):
    in_specs = (P("orb", "fft", None), P("fft", None), P("orb", None, None), P("orb", None))
    out_specs = P("orb", "fft", None)
    return jax.shard_map(
        on_device, mesh=mesh, in_specs=in_specs, out_specs=out_specs, check_vma=False
    )
```

profile of v0, /device:TPU:13, one launch (start us, length us, event | category | flops | bytes accessed | tf_op | source)
XLA Modules:
  0.0 249.2 jit_solution(12811608232977028805)
XLA Ops:
  0.0 0.8 copy.136
  0.9 0.8 copy.135
  2.2 10.2 %all_to_all.55 = s32[16,1,2]{2,1,0:T(1,128)S(1)} all-to-all(s32[16,1,2]{2,1,0:T(1,128)S(1)} %bitcast.111), channel_id=1, replica_groups=mesh['orb'=16,'fft'=2] {'orb'}, dimensions={0} | all-to-all | bytes 256 | tf_op jit(solution)/shard_map/all_to_all | solution.py:59
  13.6 1.7 select_select_fusion
  15.3 6.3 %all-to-all-start.1 = ((bf16[16,2,128,256]{3,2,1,0:T(8,128)(2,1)}), bf16[16,2,128,256]{3,2,1,0:T(8,128)(2,1)S(1)}, u32[]{:S(2)}, u32[]{:S(2)}) async-start(bf16[16,2,128,256]{3,2,1,0:T(8,128)(2,1)} %select_select_fusion), calls=%async_computation.1 | async-start | bytes 4194304 | tf_op jit(solution)/shard_map/all_to_all | solution.py:65
  22.1 47.0 %all-to-all-done.1 = bf16[16,2,128,256]{3,2,1,0:T(8,128)(2,1)S(1)} async-done(((bf16[16,2,128,256]{3,2,1,0:T(8,128)(2,1)}), bf16[16,2,128,256]{3,2,1,0:T(8,128)(2,1)S(1)}, u32[]{:S(2)}, u32[]{:S(2)}) %all-to-all-start.1) | async-done | bytes 2097184 | tf_op jit(solution)/shard_map/all_to_all | solution.py:65
  69.1 1.6 gather_fusion.1
  70.7 1.4 select_convert_fusion
  72.1 1.1 multiply_bitcast_fusion
  73.3 4.4 %all-to-all-start.2 = ((f32[8,128,256]{2,1,0:T(8,128)}), f32[8,128,256]{2,1,0:T(8,128)}, u32[]{:S(2)}, u32[]{:S(2)}) async-start(f32[8,128,256]{2,1,0:T(8,128)} %multiply_bitcast_fusion), calls=%async_computation.2 | async-start | bytes 2097152 | tf_op jit(solution)/shard_map/all_to_all | solution.py:21
  77.7 16.4 %all_gather.3 = f32[256,256]{1,0:T(8,128)S(1)} all-gather(f32[128,256]{1,0:T(8,128)S(1)} %copy-done.1), channel_id=1, replica_groups=mesh['orb'=16,'fft'=2] {'fft'}, dimensions={0}, use_global_device_ids=true | all-gather | bytes 393216 | tf_op jit(solution)/shard_map/all_gather | solution.py:22
  94.2 1.3 copy.147
  95.5 2.0 convolution_negate_fusion.1
  97.5 2.0 fusion.22
  99.4 2.0 fusion.24
  101.4 2.0 fusion.18
  103.5 2.0 fusion.6
  105.5 2.2 fusion.10
  107.7 2.0 fusion.26
  109.7 2.0 fusion.4
  111.7 2.0 fusion.2
  113.7 2.0 fusion.1
  115.8 2.0 fusion.20
  117.7 2.2 fusion
  120.6 15.2 %all_to_all.56 = f32[4,256,256]{2,0,1:T(4,128)S(1)} all-to-all(f32[4,256,256]{2,0,1:T(4,128)S(1)} %copy.156), channel_id=1, replica_groups=mesh['orb'=16,'fft'=2] {'fft'}, dimensions={1} | all-to-all | bytes 2097152 | tf_op jit(solution)/shard_map/all_to_all | solution.py:38
  136.6 2.5 broadcast_in_dim.63
  139.1 3.7 %scatter_fusion = f32[32,128,256]{2,1,0:T(8,128)} fusion(f32[32,128,256]{2,1,0:T(8,128)} %broadcast_in_dim.63, s32[16]{0:T(128)S(1)} %fusion.47, f32[16,128,256]{2,1,0:T(8,128)S(1)} %bitcast.103), kind=kCustom, calls=%fused_computation.2 | custom fusion | bytes 6291520 | tf_op jit(solution)/shard_map/scatter | solution.py:79
  142.8 6.5 %all-to-all-start.4 = ((f32[16,2,128,256]{3,2,1,0:T(8,128)}), f32[16,2,128,256]{3,2,1,0:T(8,128)}, u32[]{:S(2)}, u32[]{:S(2)}) async-start(f32[16,2,128,256]{3,2,1,0:T(8,128)} %bitcast.99), calls=%async_computation.4 | async-start | bytes 8388608 | tf_op jit(solution)/shard_map/all_to_all | solution.py:82
  150.5 91.2 %all-to-all-done.4 = f32[16,2,128,256]{3,2,1,0:T(8,128)} async-done(((f32[16,2,128,256]{3,2,1,0:T(8,128)}), f32[16,2,128,256]{3,2,1,0:T(8,128)}, u32[]{:S(2)}, u32[]{:S(2)}) %all-to-all-start.4) | async-done | bytes 4194336 | tf_op jit(solution)/shard_map/all_to_all | solution.py:82
  241.7 4.6 %copy.178 = f32[4,8,128,256]{3,1,2,0:T(8,128)S(1)} copy(f32[4,8,128,256]{3,2,1,0:T(8,128)} %bitcast.44) | data formatting | bytes 8388608
  246.3 1.6 convolution_negate_fusion
  247.9 1.3 copy.161
  (44 shorter events, 5.1 us)
Async XLA Ops:
  0.0 12.9 %copy-start = (bf16[8,128,256]{2,1,0:T(8,128)(2,1)S(1)}, bf16[8,128,256]{2,1,0:T(8,128)(2,1)}, u32[]{:S(2)}) copy-start(bf16[8,128,256]{2,1,0:T(8,128)(2,1)} %param.4) | copy-start | bytes 1572868
  15.3 6.4 %copy-start.2 = (s32[8,2,1]{0,2,1:T(1,128)S(1)}, s32[8,2,1]{0,2,1:T(1,128)}, u32[]{:S(2)}) copy-start(s32[8,2,1]{0,2,1:T(1,128)} %param.6) | copy-start | bytes 196
  15.3 53.8 %all-to-all-start.1 = ((bf16[16,2,128,256]{3,2,1,0:T(8,128)(2,1)}), bf16[16,2,128,256]{3,2,1,0:T(8,128)(2,1)S(1)}, u32[]{:S(2)}, u32[]{:S(2)}) async-start(bf16[16,2,128,256]{3,2,1,0:T(8,128)(2,1)} %select_select_fusion), calls=%async_computation.1 | async-start | bytes 4194304 | tf_op jit(solution)/shard_map/all_to_all | solution.py:65
  72.1 5.6 %copy-start.1 = (f32[128,256]{1,0:T(8,128)S(1)}, f32[128,256]{1,0:T(8,128)}, u32[]{:S(2)}) copy-start(f32[128,256]{1,0:T(8,128)} %param.5) | copy-start | bytes 393220
  73.3 20.9 %all-to-all-start.2 = ((f32[8,128,256]{2,1,0:T(8,128)}), f32[8,128,256]{2,1,0:T(8,128)}, u32[]{:S(2)}, u32[]{:S(2)}) async-start(f32[8,128,256]{2,1,0:T(8,128)} %multiply_bitcast_fusion), calls=%async_computation.2 | async-start | bytes 2097152 | tf_op jit(solution)/shard_map/all_to_all | solution.py:21
  142.8 98.9 %all-to-all-start.4 = ((f32[16,2,128,256]{3,2,1,0:T(8,128)}), f32[16,2,128,256]{3,2,1,0:T(8,128)}, u32[]{:S(2)}, u32[]{:S(2)}) async-start(f32[16,2,128,256]{3,2,1,0:T(8,128)} %bitcast.99), calls=%async_computation.4 | async-start | bytes 8388608 | tf_op jit(solution)/shard_map/all_to_all | solution.py:82
where the time goes:
time: 250 us; the launch traced here: 249 us
  waiting for transfers between devices  138 us (55%)
  blocking collectives  41.7 us (17%)
  matrix products  25.9 us (10%)
  local copies, waits for them, and re-layouts  20 us (8%)
  starting transfers between devices  17.2 us (7%)
  other arithmetic  5.88 us (2%)
    all_to_all x1, waiting for transfers between devices, on_device(): lax.all_to_all(outgoing, 'orb', split_axis=0, concat_axis=0, tiled=True)  91.2 us
    all_to_all x1, waiting for transfers between devices, on_device(): lax.all_to_all(served, 'orb', split_axis=0, concat_axis=0, tiled=True)  47 us
    dot_general x12, matrix products, product(): return jnp.einsum(form, left, right, precision=lax.Precision.HIGHEST)  24.4 us
    all_gather x1, blocking collectives, group_potential(): whole = lax.all_gather(kernel, 'fft', axis=0, tiled=True)  16.4 us
    all_to_all x1, blocking collectives, group_potential(): lax.all_to_all(spread, 'fft', split_axis=1, concat_axis=0, tiled=True)  15.2 us
    all_to_all x1, blocking collectives, on_device(): lax.all_to_all(wanted, 'orb', split_axis=0, concat_axis=0, tiled=True)  10.2 us
    all_to_all x1, starting transfers between devices, on_device(): lax.all_to_all(outgoing, 'orb', split_axis=0, concat_axis=0, tiled=True)  6.47 us
    all_to_all x1, starting transfers between devices, on_device(): lax.all_to_all(served, 'orb', split_axis=0, concat_axis=0, tiled=True)  6.35 us
  transfers between devices with their start and end apart: 3, of which 2 were waited for; matrix products, arithmetic and copies ran while one was open for 1% of the time, Pallas kernels for 0%

commit v1 on v0

v1 whole, which is shorter than its diff:
```python
import math

import jax
import jax.numpy as jnp
import numpy as np
from jax import lax
from jax.sharding import PartitionSpec as P

LEVELS = 32767.0
STEPS = 128.0
LANES = 128


def angles(length):
    series = np.arange(length)
    return (series[:, None] * series[None, :] % length) * (2.0 * math.pi / length)


def packed_tables(length):
    half = length // 2
    angle = angles(length)[:, :half]
    sine = np.sin(angle)
    sine[:, 0] = np.cos(math.pi * np.arange(length))
    forward = np.concatenate([np.cos(angle), sine], axis=1)
    gain = np.full((2 * half,), 2.0)
    gain[0] = gain[half] = 1.0
    backward = (forward * gain).T
    return forward.astype(np.float32), backward.astype(np.float32)


def product(form, left, right):
    return jnp.einsum(form, left, right, precision=lax.Precision.HIGH, preferred_element_type=jnp.float32)


def weights(kernel):
    half = kernel.shape[0] // 2
    mirror = jnp.roll(jnp.flip(kernel, (0, 1)), 1, (0, 1))
    even = (0.5 * (kernel + mirror)).T
    plus = even[:, :half]
    minus = jnp.concatenate([even[:, half : half + 1], even[:, 1:half]], axis=1)
    return plus, minus


def convolve(density, kernel):
    full_x, width_y = density.shape[1:]
    half = width_y // 2
    forward, backward = packed_tables(width_y)
    angle = angles(full_x)
    both = np.concatenate([np.cos(angle), np.sin(angle)], axis=0).astype(np.float32)
    plus, minus = weights(kernel)
    scale = 1.0 / (full_x * width_y)
    weight = jnp.concatenate([plus, minus], axis=1) * scale
    spread = product("txy,yk->txk", density, forward)
    mixed = product("qx,txk->tqk", both, spread)
    cos_part = mixed[:, :full_x] * weight
    sin_part = mixed[:, full_x:] * weight
    first = cos_part[:, :, :half] - sin_part[:, :, half:]
    second = sin_part[:, :, :half] + cos_part[:, :, half:]
    back = product("qx,txk->tqk", both, jnp.concatenate([first, second], axis=2))
    cos_part = back[:, :full_x]
    sin_part = back[:, full_x:]
    real = cos_part[:, :, :half] + sin_part[:, :, half:]
    imag = cos_part[:, :, half:] - sin_part[:, :, :half]
    return product("txk,ky->txy", jnp.concatenate([real, imag], axis=2), backward)


def encode(values, run):
    rows, width = values.shape
    runs = values.reshape(rows, width // run, run)
    peak = jnp.maximum(jnp.max(jnp.abs(runs), axis=2), 1e-30)
    level = jnp.ceil(jnp.log2(peak) * STEPS + 0.01)
    rate = jnp.exp2(level / STEPS)
    coded = jnp.round(runs * (LEVELS / rate)[:, :, None]).reshape(rows, width)
    extra = jnp.pad(level, ((0, 0), (0, LANES - width // run)))
    return jnp.concatenate([coded, extra], axis=1).astype(jnp.int16)


def decode(coded, run):
    rows = coded.shape[0]
    width = coded.shape[1] - LANES
    level = coded[:, width : width + width // run].astype(jnp.float32)
    rate = jnp.exp2(level / STEPS) / LEVELS
    runs = coded[:, :width].astype(jnp.float32).reshape(rows, width // run, run)
    return (runs * rate[:, :, None]).reshape(rows, width)


def on_device(orbitals, kernel, partner_owner, partner_local):
    peers = lax.axis_size("orb")
    parts = lax.axis_size("fft")
    orb_dev, rows_x, width_y = orbitals.shape
    tasks_dev = partner_local.shape[0]
    tasks = tasks_dev * peers
    norb = orb_dev * peers
    full_x = rows_x * parts
    chunk = rows_x * width_y // peers
    run = min(width_y, chunk)
    own = tasks // (peers * parts)

    whole = lax.all_to_all(
        jnp.broadcast_to(kernel[None], (parts,) + kernel.shape), "fft", 0, 0, tiled=True
    ).reshape(parts * kernel.shape[0], kernel.shape[1])
    named = partner_owner[:, :, 0] * orb_dev + partner_local
    named = jnp.broadcast_to(named[None], (peers, tasks_dev, 2))
    pair_ids = lax.all_to_all(named, "orb", 0, 0, tiled=True).reshape(tasks, 2)
    held = lax.all_to_all(
        orbitals.reshape(orb_dev, peers, chunk).transpose(1, 0, 2), "orb", 0, 0, tiled=True
    ).reshape(norb, chunk)

    pick = (pair_ids.T.reshape(2 * tasks, 1) == jnp.arange(norb, dtype=jnp.int32)[None, :]).astype(jnp.bfloat16)
    chosen = jnp.dot(pick, held, preferred_element_type=jnp.float32)
    first, second = chosen[:tasks], chosen[tasks:]
    density = first * second

    sent = encode(density, run).reshape(parts, peers, own, chunk + LANES)
    got = lax.all_to_all(sent.reshape(parts * peers * own, chunk + LANES), ("fft", "orb"), 0, 0, tiled=True)
    grid = decode(got, run).reshape(parts * peers, own, chunk)
    grid = grid.transpose(1, 0, 2).reshape(own, full_x, width_y)
    potential = convolve(grid, whole)
    potential = potential.reshape(own, parts * peers, chunk).transpose(1, 0, 2)
    sent = encode(potential.reshape(parts * peers * own, chunk), run)
    got = lax.all_to_all(sent, ("fft", "orb"), 0, 0, tiled=True)
    potential = decode(got, run)

    terms = jnp.concatenate([potential * second, potential * first], axis=0)
    high = lax.reduce_precision(terms, 8, 7)
    low = (terms - high).astype(jnp.bfloat16)
    high = high.astype(jnp.bfloat16)
    total = jnp.einsum(
        "to,tc->oc",
        jnp.concatenate([pick, pick], axis=0),
        jnp.concatenate([high, low], axis=0),
        preferred_element_type=jnp.float32,
    )
    sent = encode(-total, run)
    got = decode(lax.all_to_all(sent, "orb", 0, 0, tiled=True), run)
    return got.reshape(peers, orb_dev, chunk).transpose(1, 0, 2).reshape(orb_dev, rows_x, width_y)


def solution(mesh):
    in_specs = (P("orb", "fft", None), P("fft", None), P("orb", None, None), P("orb", None))
    out_specs = P("orb", "fft", None)
    return jax.shard_map(
        on_device, mesh=mesh, in_specs=in_specs, out_specs=out_specs, check_vma=False
    )
```

time: 250 us -> 146 us (0.58)
  the two profiles are of different devices: /device:TPU:13 before, /device:TPU:0 now
where the time goes in v1:
time: 146 us; the launch traced here: 145 us
  waiting for transfers between devices  51.6 us (35%)
  local copies, waits for them, and re-layouts  29.3 us (20%)
  starting transfers between devices  20.9 us (14%)
  blocking collectives  19.7 us (13%)
  other arithmetic  16.3 us (11%)
  matrix products  6.63 us (5%)
    all_to_all x1, blocking collectives, on_device(): got = decode(lax.all_to_all(sent, 'orb', 0, 0, tiled=True), run)  19.7 us
    all_to_all x1, waiting for transfers between devices, on_device(): got = lax.all_to_all(sent, ('fft', 'orb'), 0, 0, tiled=True)  16.2 us
    all_to_all x1, waiting for transfers between devices, on_device(): lax.all_to_all(sent.reshape(parts * peers * own, chunk + LANES), ('fft',...  15 us
    all_to_all x1, waiting for transfers between devices, on_device(): lax.all_to_all(orbitals.reshape(orb_dev, peers, chunk).transpose(1, 0, 2)...  14.1 us
    all_to_all x1, starting transfers between devices, on_device(): pair_ids = lax.all_to_all(named, 'orb', 0, 0, tiled=True).reshape(tasks, 2)  7.41 us
    dot_general x4, matrix products, product(): jnp.einsum(form, left, right, precision=lax.Precision.HIGH, preferred_ele...  5.66 us
    mul x4, local copies, waits for them, and re-layouts, encode(): coded = jnp.round(runs * (LEVELS / rate)[:, :, None]).reshape(rows, width)  4.25 us
    all_to_all x1, waiting for transfers between devices, on_device(): pair_ids = lax.all_to_all(named, 'orb', 0, 0, tiled=True).reshape(tasks, 2)  4.13 us
  transfers between devices with their start and end apart: 5, of which 5 were waited for; matrix products, arithmetic and copies ran while one was open for 5% of the time, Pallas kernels for 0%

profile of v1, /device:TPU:0, one launch (start us, length us, event | category | flops | bytes accessed | tf_op | source)
XLA Modules:
  0.0 144.9 jit_solution(17456303738112981096)
XLA Ops:
  2.0 7.4 %all-to-all-start = ((s32[16,8,2]{1,2,0:T(2,128)}), s32[16,8,2]{1,2,0:T(2,128)S(1)}, u32[]{:S(2)}, u32[]{:S(2)}) async-start(s32[16,8,2]{1,2,0:T(2,128)} %broadcast_in_dim.4), calls=%async_computation | async-start | bytes 32768 | tf_op jit(solution)/shard_map/all_to_all | solution.py:104
  9.4 1.3 reshape.125
  10.7 1.1 copy.81
  11.8 4.1 %all-to-all-done = s32[16,8,2]{1,2,0:T(2,128)S(1)} async-done(((s32[16,8,2]{1,2,0:T(2,128)}), s32[16,8,2]{1,2,0:T(2,128)S(1)}, u32[]{:S(2)}, u32[]{:S(2)}) %all-to-all-start) | async-done | bytes 1056 | tf_op jit(solution)/shard_map/all_to_all | solution.py:104
  15.9 3.6 %all-to-all-start.1 = ((bf16[16,8,2048]{2,1,0:T(8,128)(2,1)}), bf16[16,8,2048]{2,1,0:T(8,128)(2,1)S(1)}, u32[]{:S(2)}, u32[]{:S(2)}) async-start(bf16[16,8,2048]{2,1,0:T(8,128)(2,1)} %copy.81), calls=%async_computation.1 | async-start | bytes 1048576 | tf_op jit(solution)/shard_map/all_to_all | solution.py:105
  19.6 14.1 %all-to-all-done.1 = bf16[16,8,2048]{2,1,0:T(8,128)(2,1)S(1)} async-done(((bf16[16,8,2048]{2,1,0:T(8,128)(2,1)}), bf16[16,8,2048]{2,1,0:T(8,128)(2,1)S(1)}, u32[]{:S(2)}, u32[]{:S(2)}) %all-to-all-start.1) | async-done | bytes 524320 | tf_op jit(solution)/shard_map/all_to_all | solution.py:105
  34.5 3.4 %all-to-all-start.3 = ((f32[2,128,256]{2,1,0:T(8,128)}), f32[2,128,256]{2,1,0:T(8,128)S(1)}, u32[]{:S(2)}, u32[]{:S(2)}) async-start(f32[2,128,256]{2,1,0:T(8,128)} %broadcast_in_dim.5), calls=%async_computation.3 | async-start | bytes 524288 | tf_op jit(solution)/shard_map/all_to_all | solution.py:99
  41.6 2.0 %all-to-all-done.3 = f32[2,128,256]{2,1,0:T(8,128)S(1)} async-done(((f32[2,128,256]{2,1,0:T(8,128)}), f32[2,128,256]{2,1,0:T(8,128)S(1)}, u32[]{:S(2)}, u32[]{:S(2)}) %all-to-all-start.3) | async-done | bytes 262176 | tf_op jit(solution)/shard_map/all_to_all | solution.py:99
  43.6 3.6 %all-to-all-start.2 = ((s16[32,4,2176]{2,1,0:T(4,128)(2,1)}), s16[32,4,2176]{2,1,0:T(4,128)(2,1)}, u32[]{:S(2)}, u32[]{:S(2)}) async-start(s16[32,4,2176]{2,1,0:T(4,128)(2,1)} %pad_add_fusion), calls=%async_computation.2 | async-start | bytes 1114112 | tf_op jit(solution)/shard_map/all_to_all | solution.py:115
  48.6 15.0 %all-to-all-done.2 = s16[32,4,2176]{2,1,0:T(4,128)(2,1)} async-done(((s16[32,4,2176]{2,1,0:T(4,128)(2,1)}), s16[32,4,2176]{2,1,0:T(4,128)(2,1)}, u32[]{:S(2)}, u32[]{:S(2)}) %all-to-all-start.2) | async-done | bytes 557088 | tf_op jit(solution)/shard_map/all_to_all | solution.py:115
  63.7 1.2 all_to_all.30
  64.9 1.1 slice_convert_fusion
  66.2 1.2 mul.143
  67.4 1.7 %mul.144 = f32[32,4,2048]{2,1,0:T(4,128)S(1)} reshape(f32[128,8,256]{2,1,0:T(8,128)} %mul.143) | data formatting | bytes 2097152 | tf_op jit(solution)/shard_map/mul | solution.py:84
  69.1 2.5 %reshape.136 = f32[32,4,2048]{2,1,0:T(4,128)} reshape(f32[128,2048]{1,0:T(8,128)} %slice_convert_fusion) | data formatting | bytes 2097152 | tf_op jit(solution)/shard_map/reshape | solution.py:83
  71.6 1.5 %multiply_bitcast_fusion = f32[4,32,2048]{2,0,1:T(4,128)S(1)} fusion(f32[32,4,2048]{2,1,0:T(4,128)} %reshape.136, f32[32,4,2048]{2,1,0:T(4,128)S(1)} %mul.144), kind=kLoop, calls=%fused_computation.27 | loop fusion | flops 262144 | bytes 3145728 | tf_op jit(solution)/shard_map/transpose | solution.py:117
  73.1 1.6 %copy.87 = f32[4,32,2048]{2,1,0:T(8,128)} copy(f32[4,32,2048]{2,0,1:T(4,128)S(1)} %multiply_bitcast_fusion) | data formatting | bytes 2097152 | tf_op jit(solution)/shard_map/transpose | solution.py:117
  74.7 1.4 reshape.129
  76.1 1.6 %fusion.34 = f32[4,256,256]{1,2,0:T(8,128)S(1)} fusion(f32[4,256,256]{2,1,0:T(8,128)S(1)} %reshape.129, f32[256,256,1]{1,0,2:T(8,128)} %constant.60), kind=kOutput, calls=%fused_computation.77 | convolution fusion | flops 402653184 | bytes 2359296 | tf_op jit(solution)/shard_map/txy,yk->txk/dot_general | solution.py:32
  81.1 2.0 %fusion.7 = f32[4,256,256]{2,1,0:T(8,128)} fusion(f32[256,256,1]{1,0,2:T(8,128)S(1)} %copy-done.1, f32[4,256,128]{1,2,0:T(8,128)S(1)} %get-tuple-element.12, f32[4,256,128]{1,2,0:T(8,128)S(1)} %get-tuple-element.11), kind=kOutput, calls=%fused_computation.15 | convolution fusion | flops 402915328 | bytes 2359296 | tf_op jit(solution)/shard_map/txk,ky->txy/dot_general | solution.py:32
  83.1 1.4 reshape.131
  84.5 1.8 %bitcast_abs_fusion = f32[32,4,2048]{2,1,0:T(4,128)} fusion(f32[4,32,2048]{2,1,0:T(8,128)S(1)} %reshape.131), kind=kLoop, calls=%fused_computation.22 | loop fusion | flops 262144 | bytes 2097152 | tf_op jit(solution)/shard_map/abs | solution.py:70
  86.3 2.7 %abs.21 = f32[128,8,256]{2,1,0:T(8,128)} reshape(f32[32,4,2048]{2,1,0:T(4,128)} %bitcast_abs_fusion) | data formatting | bytes 2097152 | tf_op jit(solution)/shard_map/abs | solution.py:70
  89.0 1.4 reduce_max.28
  90.7 1.2 mul.154
  91.8 2.7 %mul.155 = f32[32,4,2048]{2,1,0:T(4,128)} reshape(f32[128,8,256]{2,1,0:T(8,128)} %mul.154) | data formatting | bytes 2097152 | tf_op jit(solution)/shard_map/mul | solution.py:73
  94.5 3.0 %fusion.13 = s16[32,4,2048]{2,1,0:T(4,128)(2,1)} fusion(f32[32,4,2048]{2,1,0:T(4,128)} %mul.155, f32[4,32,2048]{2,1,0:T(8,128)S(1)} %reshape.131), kind=kLoop, calls=%fused_computation.24 | loop fusion | flops 786432 | bytes 2621440 | tf_op jit(solution)/shard_map/convert.9
  97.7 2.1 %pad_add_fusion.1 = s16[32,4,2176]{2,1,0:T(4,128)(2,1)} fusion(s16[32,4,128]{2,1,0:T(4,128)(2,1)S(1)} %bitcast.75, s16[32,4,2048]{2,1,0:T(4,128)(2,1)} %fusion.13), kind=kLoop, calls=%fused_computation.33 | loop fusion | flops 278528 | bytes 1114112 | tf_op jit(solution)/shard_map/concatenate | solution.py:75
  99.8 2.8 %all-to-all-start.4 = ((s16[32,4,2176]{2,1,0:T(4,128)(2,1)}), s16[32,4,2176]{2,1,0:T(4,128)(2,1)S(1)}, u32[]{:S(2)}, u32[]{:S(2)}) async-start(s16[32,4,2176]{2,1,0:T(4,128)(2,1)} %pad_add_fusion.1), calls=%async_computation.4 | async-start | bytes 1114112 | tf_op jit(solution)/shard_map/all_to_all | solution.py:121
  102.7 16.2 %all-to-all-done.4 = s16[32,4,2176]{2,1,0:T(4,128)(2,1)S(1)} async-done(((s16[32,4,2176]{2,1,0:T(4,128)(2,1)}), s16[32,4,2176]{2,1,0:T(4,128)(2,1)S(1)}, u32[]{:S(2)}, u32[]{:S(2)}) %all-to-all-start.4) | async-done | bytes 557088 | tf_op jit(solution)/shard_map/all_to_all | solution.py:121
  122.7 19.7 %all_to_all.42 = s16[16,8,2176]{2,1,0:T(8,128)(2,1)S(1)} all-to-all(s16[16,8,2176]{2,1,0:T(8,128)(2,1)S(1)} %pad_add_fusion.2), channel_id=1, replica_groups=mesh['orb'=16,'fft'=2] {'orb'}, dimensions={0} | all-to-all | bytes 1114112 | tf_op jit(solution)/shard_map/all_to_all | solution.py:135
  143.8 1.1 reshape.134
  (79 shorter events, 16.6 us)
Async XLA Ops:
  0.0 33.8 %copy-start.2 = (f32[128,256]{1,0:T(8,128)S(1)}, f32[128,256]{1,0:T(8,128)}, u32[]{:S(2)}) copy-start(f32[128,256]{1,0:T(8,128)} %param.9) | copy-start | bytes 393220
  2.0 13.9 %all-to-all-start = ((s32[16,8,2]{1,2,0:T(2,128)}), s32[16,8,2]{1,2,0:T(2,128)S(1)}, u32[]{:S(2)}, u32[]{:S(2)}) async-start(s32[16,8,2]{1,2,0:T(2,128)} %broadcast_in_dim.4), calls=%async_computation | async-start | bytes 32768 | tf_op jit(solution)/shard_map/all_to_all | solution.py:104
  15.9 17.8 %all-to-all-start.1 = ((bf16[16,8,2048]{2,1,0:T(8,128)(2,1)}), bf16[16,8,2048]{2,1,0:T(8,128)(2,1)S(1)}, u32[]{:S(2)}, u32[]{:S(2)}) async-start(bf16[16,8,2048]{2,1,0:T(8,128)(2,1)} %copy.81), calls=%async_computation.1 | async-start | bytes 1048576 | tf_op jit(solution)/shard_map/all_to_all | solution.py:105
  34.5 9.2 %all-to-all-start.3 = ((f32[2,128,256]{2,1,0:T(8,128)}), f32[2,128,256]{2,1,0:T(8,128)S(1)}, u32[]{:S(2)}, u32[]{:S(2)}) async-start(f32[2,128,256]{2,1,0:T(8,128)} %broadcast_in_dim.5), calls=%async_computation.3 | async-start | bytes 524288 | tf_op jit(solution)/shard_map/all_to_all | solution.py:99
  43.6 20.0 %all-to-all-start.2 = ((s16[32,4,2176]{2,1,0:T(4,128)(2,1)}), s16[32,4,2176]{2,1,0:T(4,128)(2,1)}, u32[]{:S(2)}, u32[]{:S(2)}) async-start(s16[32,4,2176]{2,1,0:T(4,128)(2,1)} %pad_add_fusion), calls=%async_computation.2 | async-start | bytes 1114112 | tf_op jit(solution)/shard_map/all_to_all | solution.py:115
  76.1 1.6 %copy-start = (f32[512,256,1]{1,0,2:T(8,128)S(1)}, f32[512,256,1]{1,0,2:T(8,128)}, u32[]{:S(2)}) copy-start(f32[512,256,1]{1,0,2:T(8,128)} %constant.61) | copy-start | bytes 1572868
  80.2 1.0 copy-start.1
  99.8 19.2 %all-to-all-start.4 = ((s16[32,4,2176]{2,1,0:T(4,128)(2,1)}), s16[32,4,2176]{2,1,0:T(4,128)(2,1)S(1)}, u32[]{:S(2)}, u32[]{:S(2)}) async-start(s16[32,4,2176]{2,1,0:T(4,128)(2,1)} %pad_add_fusion.1), calls=%async_computation.4 | async-start | bytes 1114112 | tf_op jit(solution)/shard_map/all_to_all | solution.py:121

commit v2 on v1

--- a/solution.py
+++ b/solution.py
@@ -1,9 +1,12 @@
+import functools
 import math
 
 import jax
 import jax.numpy as jnp
 import numpy as np
 from jax import lax
+from jax.experimental import pallas as pl
+from jax.experimental.pallas import tpu as pltpu
 from jax.sharding import PartitionSpec as P
 
 LEVELS = 32767.0
@@ -84,7 +87,7 @@
     return (runs * rate[:, :, None]).reshape(rows, width)
 
 
-def on_device(orbitals, kernel, partner_owner, partner_local):
+def plain_device(orbitals, kernel, partner_owner, partner_local):
     peers = lax.axis_size("orb")
     parts = lax.axis_size("fft")
     orb_dev, rows_x, width_y = orbitals.shape
@@ -136,6 +139,305 @@
     return got.reshape(peers, orb_dev, chunk).transpose(1, 0, 2).reshape(orb_dev, rows_x, width_y)
 
 
+F32 = jnp.float32
+BF16 = jnp.bfloat16
+MESH = pl.DeviceIdType.MESH
+
+
+def split(values):
+    high = values.astype(BF16)
+    return high, (values - high.astype(F32)).astype(BF16)
+
+
+def dot(left, right):
+    return jnp.dot(left, right, preferred_element_type=F32)
+
+
+def left_table(table, values):
+    high, low = split(values)
+    return dot(table[0], high) + dot(table[0], low) + dot(table[1], high)
+
+
+def right_table(values, table):
+    high, low = split(values)
+    return dot(high, table[0]) + dot(low, table[0]) + dot(high, table[1])
+
+
+def iota(shape, axis):
+    return lax.broadcasted_iota(jnp.int32, shape, axis)
+
+
+def quantize(values, first_row=0):
+    count, rows, _ = values.shape
+    peak = jnp.maximum(jnp.max(jnp.abs(values), axis=2, keepdims=True), 1e-30)
+    coded = jnp.round(values * (LEVELS / peak)).astype(jnp.int32).astype(jnp.int16)
+    shape = (count, rows, LANES)
+    spot = iota(shape, 2) == iota(shape, 1) + first_row
+    scale = jnp.sum(jnp.where(spot, peak * (1.0 / LEVELS), 0.0), axis=1, keepdims=True)
+    return coded, scale
+
+
+def restore(coded, scale, first_row=0):
+    count, rows, _ = coded.shape
+    shape = (count, rows, LANES)
+    spot = iota(shape, 2) == iota(shape, 1) + first_row
+    rate = jnp.sum(jnp.where(spot, jnp.broadcast_to(scale, shape), 0.0), axis=2, keepdims=True)
+    return coded.astype(jnp.int32).astype(F32) * rate
+
+
+def half_roll(values):
+    parts = [
+        pltpu.roll(values[:, at : at + LANES], LANES // 2, 1) for at in range(0, values.shape[1], LANES)
+    ]
+    return jnp.concatenate(parts, axis=1)
+
+
+def fused(
+    peers, parts, rows, orb_dev, task_dev,
+    orb_ref, ids_ref, ker_ref, fwd_ref, bwd_ref, both_ref, out_ref,
+    held, names, whole, chosen, snd1, rec1, sc_snd1, sc_rec1, snd2, rec2, sc_snd2, sc_rec2,
+    terms, snd3, rec3, sc_snd3, sc_rec3, send_sem, recv_sem,
+):
+    o = lax.axis_index("orb")
+    f = lax.axis_index("fft")
+    everyone = peers * parts
+    me = f * peers + o
+    block = task_dev * rows
+    tasks = task_dev * peers
+    width = orb_ref.shape[2]
+    half = width // 2
+    full_x = ker_ref.shape[2]
+
+    barrier = pltpu.get_barrier_semaphore()
+
+    def greet(i, c):
+        p = lax.rem(me + i, everyone)
+        pl.semaphore_signal(barrier, inc=1, device_id=(lax.rem(p, peers), p // peers), device_id_type=MESH)
+        return c
+
+    lax.fori_loop(1, everyone, greet, 0)
+    pl.semaphore_wait(barrier, everyone - 1)
+
+    def remote(src, dst, k, device):
+        return pltpu.make_async_remote_copy(
+            src_ref=src, dst_ref=dst, send_sem=send_sem.at[k], recv_sem=recv_sem.at[k],
+            device_id=device, device_id_type=MESH,
+        )
+
+    def over_orb(src, dst, k, fixed=False):
+        def one(i, c):
+            p = lax.rem(o + i, peers)
+            remote(src if fixed else src.at[p], dst.at[o], k, (p, f)).start()
+            return c
+
+        pltpu.make_async_copy(src if fixed else src.at[o], dst.at[o], recv_sem.at[k]).start()
+        lax.fori_loop(1, peers, one, 0)
+
+    def over_all(src, dst, k):
+        def one(i, c):
+            p = lax.rem(me + i, everyone)
+            remote(src.at[p], dst.at[me], k, (lax.rem(p, peers), p // peers)).start()
+            return c
+
+        pltpu.make_async_copy(src.at[me], dst.at[me], recv_sem.at[k]).start()
+        lax.fori_loop(1, everyone, one, 0)
+
+    def arrived(dst, k):
+        pltpu.make_async_copy(dst, dst, recv_sem.at[k]).wait()
+
+    def left(dst, k):
+        gone = dst.at[pl.ds(0, dst.shape[0] - 1)]
+        pltpu.make_async_copy(gone, gone, send_sem.at[k]).wait()
+
+    over_orb(ids_ref, names, 0, fixed=True)
+    over_orb(orb_ref, held, 1)
+
+    def halves(i, c):
+        p = lax.rem(f + i, parts)
+        remote(ker_ref.at[0], whole.at[f], 2, (o, p)).start()
+        return c
+
+    pltpu.make_async_copy(ker_ref.at[0], whole.at[f], recv_sem.at[2]).start()
+    lax.fori_loop(1, parts, halves, 0)
+
+    arrived(whole, 2)
+    per = half // parts
+    turned = split(whole[...].reshape(width, full_x).T)
+    lane = iota((width, LANES), 1)
+    freq = f * per + lax.rem(lane, per)
+    freq = jnp.where((lane >= per) & (freq == 0), half, freq)
+    row = iota((width, LANES), 0)
+    straight = (row == freq).astype(F32).astype(BF16)
+    mirror = (row == lax.rem(width - freq, width)).astype(F32).astype(BF16)
+    flip_shape = (full_x, full_x)
+    flip = (iota(flip_shape, 1) == lax.rem(full_x - iota(flip_shape, 0), full_x)).astype(F32).astype(BF16)
+    plain = dot(turned[0], straight) + dot(turned[1], straight)
+    other = split(dot(turned[0], mirror) + dot(turned[1], mirror))
+    weight = (plain + dot(flip, other[0]) + dot(flip, other[1])) * (0.5 / (full_x * width))
+    sign = jnp.where(iota((full_x, 2 * LANES), 1) % LANES < per, 1.0, -1.0)
+    weight = jnp.concatenate([weight, weight], axis=1)
+    signed = weight * sign
+
+    arrived(names, 0)
+    named = names[...].reshape(tasks, LANES)
+    grow = (iota((tasks * rows, tasks), 0) // rows == iota((tasks * rows, tasks), 1)).astype(F32).astype(BF16)
+    down = dot(grow, named.astype(BF16)).astype(jnp.int32) * rows + iota((tasks * rows, LANES), 0) % rows
+    spread = (iota((tasks, tasks * rows), 1) // rows == iota((tasks, tasks * rows), 0)).astype(F32).astype(BF16)
+    across = dot(named.T[:8].astype(BF16), spread).astype(jnp.int32) * rows + iota((8, tasks * rows), 1) % rows
+
+    arrived(held, 1)
+    total_rows = tasks * rows
+    norb_rows = peers * orb_dev * rows
+    step = 4 * block
+    blocks = total_rows // step
+
+    source = held[...].reshape(norb_rows, width)
+    for b in range(blocks):
+        at = slice(b * step, (b + 1) * step)
+        pair = []
+        for c in range(2):
+            hot = (down[at, c : c + 1] == iota((step, norb_rows), 1)).astype(F32).astype(BF16)
+            value = dot(hot, source)
+            chosen[c, at, :] = value.astype(BF16)
+            pair.append(value)
+        waves = right_table(pair[0] * pair[1], fwd_ref)
+        for h in range(parts):
+            coded, scale = quantize(waves[:, h * LANES : (h + 1) * LANES].reshape(4, block, LANES))
+            snd1[h * peers + 4 * b : h * peers + 4 * b + 4] = coded
+            sc_snd1[h * peers + 4 * b : h * peers + 4 * b + 4] = scale
+    over_all(sc_snd1, sc_rec1, 3)
+    over_all(snd1, rec1, 4)
+
+    arrived(sc_rec1, 3)
+    arrived(rec1, 4)
+    scales = sc_rec1[...]
+    sent = jnp.zeros((everyone, 1, LANES), F32)
+    for i in range(task_dev // 2):
+        at = slice(2 * rows * i, 2 * rows * (i + 1))
+        values = restore(rec1[:, at, :], scales, 2 * rows * i)
+        grid = jnp.concatenate(
+            [values[:, :rows].reshape(full_x, LANES), values[:, rows:].reshape(full_x, LANES)], axis=1
+        )
+        mixed = left_table(both_ref, grid)
+        mixed = mixed[:full_x] * weight + half_roll(mixed[full_x:] * signed)
+        mixed = left_table(both_ref, mixed)
+        mixed = mixed[:full_x] + half_roll(mixed[full_x:]) * sign
+        values = jnp.concatenate(
+            [mixed[:, :LANES].reshape(everyone, rows, LANES), mixed[:, LANES:].reshape(everyone, rows, LANES)],
+            axis=1,
+        )
+        coded, scale = quantize(values, 2 * rows * i)
+        snd2[:, at, :] = coded
+        sent = sent + scale
+    sc_snd2[...] = sent
+    over_all(sc_snd2, sc_rec2, 5)
+    over_all(snd2, rec2, 6)
+
+    arrived(sc_rec2, 5)
+    arrived(rec2, 6)
+    for b in range(blocks):
+        at = slice(b * step, (b + 1) * step)
+        waves = []
+        for h in range(parts):
+            spot = slice(h * peers + 4 * b, h * peers + 4 * b + 4)
+            waves.append(restore(rec2[spot], sc_rec2[spot]).reshape(step, LANES))
+        potential = right_table(jnp.concatenate(waves, axis=1), bwd_ref)
+        for c in range(2):
+            high, low = split(potential * chosen[1 - c, at, :].astype(F32))
+            to = slice(c * total_rows + b * step, c * total_rows + (b + 1) * step)
+            terms[0, to, :] = high
+            terms[1, to, :] = low
+    ids_row = jnp.concatenate([across[0:1], across[1:2]], axis=1)
+    for b in range(norb_rows // step):
+        hot = (ids_row == iota((step, 2 * total_rows), 0) + b * step).astype(F32).astype(BF16)
+        total = -(dot(hot, terms[0]) + dot(hot, terms[1]))
+        coded, scale = quantize(total.reshape(4, block, width))
+        snd3[4 * b : 4 * b + 4] = coded
+        sc_snd3[4 * b : 4 * b + 4] = scale
+    over_orb(sc_snd3, sc_rec3, 7)
+    over_orb(snd3, rec3, 8)
+    arrived(sc_rec3, 7)
+    arrived(rec3, 8)
+    for p in range(peers):
+        values = restore(rec3[p : p + 1], sc_rec3[p : p + 1]).reshape(orb_dev, rows, width)
+        out_ref[:, p * rows : (p + 1) * rows, :] = values
+
+    left(names, 0)
+    left(held, 1)
+    gone = whole.at[pl.ds(0, parts - 1)]
+    pltpu.make_async_copy(gone, gone, send_sem.at[2]).wait()
+    left(sc_snd1, 3)
+    left(snd1, 4)
+    left(sc_snd2, 5)
+    left(snd2, 6)
+    left(sc_snd3, 7)
+    left(snd3, 8)
+
+
+def tables_of(array):
+    exact = jnp.asarray(array, F32)
+    high = lax.reduce_precision(exact, 8, 7)
+    return jnp.stack([high.astype(BF16), (exact - high).astype(BF16)])
+
+
+def fused_device(orbitals, kernel, partner_owner, partner_local):
+    peers = lax.axis_size("orb")
+    parts = lax.axis_size("fft")
+    orb_dev, rows_x, width = orbitals.shape
+    task_dev = partner_local.shape[0]
+    rows = rows_x // peers
+    full_x = rows_x * parts
+    everyone = peers * parts
+    block = orb_dev * rows
+    half = width // 2
+    per = half // parts
+
+    named = (partner_owner[:, :, 0] * orb_dev + partner_local).astype(F32)
+    named = jnp.pad(named, ((0, 0), (0, LANES - 2)))
+    sent = orbitals.reshape(orb_dev, peers, rows, width).transpose(1, 0, 2, 3).reshape(peers, block, width)
+    forward, backward = packed_tables(width)
+    order = np.concatenate(
+        [np.concatenate([np.arange(h * per, (h + 1) * per), half + np.arange(h * per, (h + 1) * per)]) for h in range(parts)]
+    )
+    angle = angles(full_x)
+    both = np.concatenate([np.cos(angle), np.sin(angle)], axis=0)
+    vmem = pl.BlockSpec(memory_space=pltpu.VMEM)
+    pieces = lambda n, w, t: [pltpu.VMEM((n, block, w), t), pltpu.VMEM((n, block, w), t)]
+    rates = lambda n: [pltpu.VMEM((n, 1, LANES), F32), pltpu.VMEM((n, 1, LANES), F32)]
+    rows_all = task_dev * peers * rows
+    return pl.pallas_call(
+        functools.partial(fused, peers, parts, rows, orb_dev, task_dev),
+        out_shape=jax.ShapeDtypeStruct((orb_dev, rows_x, width), F32),
+        in_specs=[vmem] * 6,
+        out_specs=vmem,
+        scratch_shapes=[
+            pltpu.VMEM((peers, block, width), BF16),
+            pltpu.VMEM((peers, task_dev, LANES), F32),
+            pltpu.VMEM((parts,) + kernel.shape, F32),
+            pltpu.VMEM((2, rows_all, width), BF16),
+            *pieces(everyone, LANES, jnp.int16), *rates(everyone),
+            *pieces(everyone, LANES, jnp.int16), *rates(everyone),
+            pltpu.VMEM((2, 2 * rows_all, width), BF16),
+            *pieces(peers, width, jnp.int16), *rates(peers),
+            pltpu.SemaphoreType.DMA((9,)),
+            pltpu.SemaphoreType.DMA((9,)),
+        ],
+        compiler_params=pltpu.CompilerParams(
+            collective_id=0, has_side_effects=True, vmem_limit_bytes=60 * 1024 * 1024
+        ),
+    )(sent, named, kernel[None], tables_of(forward[:, order]), tables_of(backward[order]), tables_of(both))
+
+
+def on_device(orbitals, kernel, partner_owner, partner_local):
+    peers = lax.axis_size("orb")
+    parts = lax.axis_size("fft")
+    orb_dev, rows_x, width = orbitals.shape
+    fits = rows_x == 8 * peers and width == LANES * parts and peers % 4 == 0
+    fits = fits and orb_dev == 8 and partner_local.shape[0] == 8 and orb_dev * peers <= LANES
+    step = fused_device if fits else plain_device
+    return step(orbitals, kernel, partner_owner, partner_local)
+
+
 def solution(mesh):
     in_specs = (P("orb", "fft", None), P("fft", None), P("orb", None, None), P("orb", None))
     out_specs = P("orb", "fft", None)

time: 146 us -> 74.6 us (0.51)
  the two profiles are of different devices: /device:TPU:0 before, /device:TPU:13 now
where the time goes in v2:
time: 74.6 us; the launch traced here: 73.9 us
  Pallas kernels  68.6 us (92%)
  local copies, waits for them, and re-layouts  5.21 us (7%)
    pallas_call x1, Pallas kernels, fused_device(): pl.pallas_call(functools.partial(fused, peers, parts, rows, orb_dev, task...  68.6 us
    unnamed x8, local copies, waits for them, and re-layouts  3.69 us

profile of v2, /device:TPU:13, one launch (start us, length us, event | category | flops | bytes accessed | tf_op | source)
XLA Modules:
  0.0 73.9 jit_solution(15912294756994857102)
XLA Ops:
  0.0 0.0 copy-start
  0.0 0.0 copy-start.2
  0.0 0.7 copy-done.2
  0.7 0.0 copy-start.1
  0.7 0.1 copy.9
  0.8 0.6 copy-done.1
  1.4 0.1 copy.10
  1.5 0.6 pad.4.ids_ref
  2.1 0.0 copy-done
  2.1 0.8 %copy_bitcast_fusion.orb_ref = bf16[16,64,256]{2,1,0:T(8,128)(2,1)} fusion(bf16[8,128,256]{2,1,0:T(8,128)(2,1)S(1)} %copy-done), kind=kLoop, calls=%fused_computation | loop fusion | bytes 1048576 | tf_op jit(solution)/shard_map/reshape | solution.py:397
  3.0 68.6 %shard_map.73 = f32[8,128,256]{2,1,0:T(8,128)} custom-call(bf16[16,64,256]{2,1,0:T(8,128)(2,1)} %copy_bitcast_fusion.orb_ref, f32[8,128]{1,0:T(8,128)} %pad.4.ids_ref, f32[1,128,256]{2,1,0:T(8,128)} %bitcast.9, bf16[2,256,256]{2,1,0:T(8,128)(2,1)} %constant.25.fwd_ref, bf16[2,256,256]{2,1,0:T(8,128)(2,1)} %constant.32.bwd_ref, ...), custom_call_target="tpu_custom_call" | custom-call | tf_op jit(solution)/shard_map/pallas_call | solution.py:408
  71.6 2.3 %copy.13 = f32[8,128,256]{2,1,0:T(8,128)} copy(f32[8,128,256]{2,1,0:T(8,128)} %shard_map.73) | data formatting | bytes 2097152
  (2 shorter events, 0.0 us)
Async XLA Ops:
  0.0 2.1 %copy-start = (bf16[8,128,256]{2,1,0:T(8,128)(2,1)S(1)}, bf16[8,128,256]{2,1,0:T(8,128)(2,1)}, u32[]{:S(2)}) copy-start(bf16[8,128,256]{2,1,0:T(8,128)(2,1)} %param.7) | copy-start | bytes 1572868
  0.0 0.7 copy-start.2
  0.7 0.7 copy-start.1

commit v3 on v2

--- a/solution.py
+++ b/solution.py
@@ -194,19 +194,24 @@
 
 def fused(
     peers, parts, rows, orb_dev, task_dev,
-    orb_ref, ids_ref, ker_ref, fwd_ref, bwd_ref, both_ref, out_ref,
+    orb_ref, ids_ref, ker_ref, fwd_ref, bwd_ref, both_ref, coded_ref, rate_ref,
     held, names, whole, chosen, snd1, rec1, sc_snd1, sc_rec1, snd2, rec2, sc_snd2, sc_rec2,
-    terms, snd3, rec3, sc_snd3, sc_rec3, send_sem, recv_sem,
+    hots, turned_hots, acc, snd3, rec3, sc_snd3, sc_rec3, send_sem, recv_sem,
 ):
     o = lax.axis_index("orb")
     f = lax.axis_index("fft")
     everyone = peers * parts
     me = f * peers + o
-    block = task_dev * rows
     tasks = task_dev * peers
     width = orb_ref.shape[2]
     half = width // 2
     full_x = ker_ref.shape[2]
+    deep = snd1.shape[2]
+    chunks = snd1.shape[0]
+    step = peers * deep
+    total_rows = tasks * rows
+    norb_rows = peers * orb_dev * rows
+    pack = deep // rows
 
     barrier = pltpu.get_barrier_semaphore()
 
@@ -233,13 +238,16 @@
         pltpu.make_async_copy(src if fixed else src.at[o], dst.at[o], recv_sem.at[k]).start()
         lax.fori_loop(1, peers, one, 0)
 
-    def over_all(src, dst, k):
-        def one(i, c):
-            p = lax.rem(me + i, everyone)
-            remote(src.at[p], dst.at[me], k, (lax.rem(p, peers), p // peers)).start()
+    def over_all(i, scale, scale_to, src, dst, k):
+        def one(j, c):
+            p = lax.rem(me + j, everyone)
+            device = (lax.rem(p, peers), p // peers)
+            remote(scale.at[i, p], scale_to.at[i, me], k + i, device).start()
+            remote(src.at[i, p], dst.at[i, me], k + chunks + i, device).start()
             return c
 
-        pltpu.make_async_copy(src.at[me], dst.at[me], recv_sem.at[k]).start()
+        pltpu.make_async_copy(scale.at[i, me], scale_to.at[i, me], recv_sem.at[k + i]).start()
+        pltpu.make_async_copy(src.at[i, me], dst.at[i, me], recv_sem.at[k + chunks + i]).start()
         lax.fori_loop(1, everyone, one, 0)
 
     def arrived(dst, k):
@@ -259,6 +267,23 @@
 
     pltpu.make_async_copy(ker_ref.at[0], whole.at[f], recv_sem.at[2]).start()
     lax.fori_loop(1, parts, halves, 0)
+
+    def task_of(row):
+        return row // deep % peers * task_dev + row // step * pack + row // rows % pack
+
+    arrived(names, 0)
+    named = names[...].reshape(tasks, LANES)
+    grow = (task_of(iota((total_rows, tasks), 0)) == iota((total_rows, tasks), 1)).astype(F32).astype(BF16)
+    down = dot(grow, named.astype(BF16)).astype(jnp.int32) * rows + iota((total_rows, LANES), 0) % rows
+    spread = (task_of(iota((tasks, total_rows), 1)) == iota((tasks, total_rows), 0)).astype(F32).astype(BF16)
+    across = dot(named.T[:8].astype(BF16), spread).astype(jnp.int32) * rows + iota((8, total_rows), 1) % rows
+    for i in range(chunks):
+        at = slice(i * step, (i + 1) * step)
+        for c in range(2):
+            hot = down[at, c : c + 1] == iota((step, norb_rows), 1)
+            hots[c, at, :] = hot.astype(F32).astype(BF16)
+            hot = across[c : c + 1, at] == iota((norb_rows, step), 0)
+            turned_hots[i, :, c * step : (c + 1) * step] = hot.astype(F32).astype(BF16)
 
     arrived(whole, 2)
     per = half // parts
@@ -274,104 +299,112 @@
     plain = dot(turned[0], straight) + dot(turned[1], straight)
     other = split(dot(turned[0], mirror) + dot(turned[1], mirror))
     weight = (plain + dot(flip, other[0]) + dot(flip, other[1])) * (0.5 / (full_x * width))
-    sign = jnp.where(iota((full_x, 2 * LANES), 1) % LANES < per, 1.0, -1.0)
-    weight = jnp.concatenate([weight, weight], axis=1)
+    sign = jnp.where(iota((full_x, pack * LANES), 1) % LANES < per, 1.0, -1.0)
+    weight = jnp.concatenate([weight] * pack, axis=1)
     signed = weight * sign
 
-    arrived(names, 0)
-    named = names[...].reshape(tasks, LANES)
-    grow = (iota((tasks * rows, tasks), 0) // rows == iota((tasks * rows, tasks), 1)).astype(F32).astype(BF16)
-    down = dot(grow, named.astype(BF16)).astype(jnp.int32) * rows + iota((tasks * rows, LANES), 0) % rows
-    spread = (iota((tasks, tasks * rows), 1) // rows == iota((tasks, tasks * rows), 0)).astype(F32).astype(BF16)
-    across = dot(named.T[:8].astype(BF16), spread).astype(jnp.int32) * rows + iota((8, tasks * rows), 1) % rows
-
     arrived(held, 1)
-    total_rows = tasks * rows
-    norb_rows = peers * orb_dev * rows
-    step = 4 * block
-    blocks = total_rows // step
-
     source = held[...].reshape(norb_rows, width)
-    for b in range(blocks):
-        at = slice(b * step, (b + 1) * step)
+    for i in range(chunks):
+        at = slice(i * step, (i + 1) * step)
         pair = []
         for c in range(2):
-            hot = (down[at, c : c + 1] == iota((step, norb_rows), 1)).astype(F32).astype(BF16)
-            value = dot(hot, source)
+            value = dot(hots[c, at, :], source)
             chosen[c, at, :] = value.astype(BF16)
             pair.append(value)
         waves = right_table(pair[0] * pair[1], fwd_ref)
         for h in range(parts):
-            coded, scale = quantize(waves[:, h * LANES : (h + 1) * LANES].reshape(4, block, LANES))
-            snd1[h * peers + 4 * b : h * peers + 4 * b + 4] = coded
-            sc_snd1[h * peers + 4 * b : h * peers + 4 * b + 4] = scale
-    over_all(sc_snd1, sc_rec1, 3)
-    over_all(snd1, rec1, 4)
-
-    arrived(sc_rec1, 3)
-    arrived(rec1, 4)
-    scales = sc_rec1[...]
-    sent = jnp.zeros((everyone, 1, LANES), F32)
-    for i in range(task_dev // 2):
-        at = slice(2 * rows * i, 2 * rows * (i + 1))
-        values = restore(rec1[:, at, :], scales, 2 * rows * i)
+            coded, scale = quantize(waves[:, h * LANES : (h + 1) * LANES].reshape(peers, deep, LANES))
+            snd1[i, h * peers : (h + 1) * peers] = coded
+            sc_snd1[i, h * peers : (h + 1) * peers] = scale
+        over_all(i, sc_snd1, sc_rec1, snd1, rec1, 3)
+
+    for i in range(chunks):
+        arrived(sc_rec1.at[i], 3 + i)
+        arrived(rec1.at[i], 3 + chunks + i)
+        values = restore(rec1[i], sc_rec1[i])
         grid = jnp.concatenate(
-            [values[:, :rows].reshape(full_x, LANES), values[:, rows:].reshape(full_x, LANES)], axis=1
+            [values[:, t * rows : (t + 1) * rows].reshape(full_x, LANES) for t in range(pack)], axis=1
         )
         mixed = left_table(both_ref, grid)
         mixed = mixed[:full_x] * weight + half_roll(mixed[full_x:] * signed)
         mixed = left_table(both_ref, mixed)
         mixed = mixed[:full_x] + half_roll(mixed[full_x:]) * sign
         values = jnp.concatenate(
-            [mixed[:, :LANES].reshape(everyone, rows, LANES), mixed[:, LANES:].reshape(everyone, rows, LANES)],
-            axis=1,
+            [mixed[:, t * LANES : (t + 1) * LANES].reshape(everyone, rows, LANES) for t in range(pack)], axis=1
         )
-        coded, scale = quantize(values, 2 * rows * i)
-        snd2[:, at, :] = coded
-        sent = sent + scale
-    sc_snd2[...] = sent
-    over_all(sc_snd2, sc_rec2, 5)
-    over_all(snd2, rec2, 6)
-
-    arrived(sc_rec2, 5)
-    arrived(rec2, 6)
-    for b in range(blocks):
-        at = slice(b * step, (b + 1) * step)
+        coded, scale = quantize(values)
+        snd2[i] = coded
+        sc_snd2[i] = scale
+        over_all(i, sc_snd2, sc_rec2, snd2, rec2, 3 + 2 * chunks)
+
+    last = 3 + 4 * chunks
+    for i in range(chunks):
+        at = slice(i * step, (i + 1) * step)
+        arrived(sc_rec2.at[i], 3 + 2 * chunks + i)
+        arrived(rec2.at[i], 3 + 3 * chunks + i)
         waves = []
         for h in range(parts):
-            spot = slice(h * peers + 4 * b, h * peers + 4 * b + 4)
-            waves.append(restore(rec2[spot], sc_rec2[spot]).reshape(step, LANES))
+            spot = slice(h * peers, (h + 1) * peers)
+            waves.append(restore(rec2[i, spot], sc_rec2[i, spot]).reshape(step, LANES))
         potential = right_table(jnp.concatenate(waves, axis=1), bwd_ref)
-        for c in range(2):
-            high, low = split(potential * chosen[1 - c, at, :].astype(F32))
-            to = slice(c * total_rows + b * step, c * total_rows + (b + 1) * step)
-            terms[0, to, :] = high
-            terms[1, to, :] = low
-    ids_row = jnp.concatenate([across[0:1], across[1:2]], axis=1)
-    for b in range(norb_rows // step):
-        hot = (ids_row == iota((step, 2 * total_rows), 0) + b * step).astype(F32).astype(BF16)
-        total = -(dot(hot, terms[0]) + dot(hot, terms[1]))
-        coded, scale = quantize(total.reshape(4, block, width))
-        snd3[4 * b : 4 * b + 4] = coded
-        sc_snd3[4 * b : 4 * b + 4] = scale
-    over_orb(sc_snd3, sc_rec3, 7)
-    over_orb(snd3, rec3, 8)
-    arrived(sc_rec3, 7)
-    arrived(rec3, 8)
-    for p in range(peers):
-        values = restore(rec3[p : p + 1], sc_rec3[p : p + 1]).reshape(orb_dev, rows, width)
-        out_ref[:, p * rows : (p + 1) * rows, :] = values
+        high, low = split(
+            jnp.concatenate([potential * chosen[1 - c, at, :].astype(F32) for c in range(2)], axis=0)
+        )
+        if i < chunks - 1:
+            term = dot(turned_hots[i], high) + dot(turned_hots[i], low)
+            acc[...] = term if i == 0 else acc[...] + term
+            continue
+        some = norb_rows // 4
+        group = peers // 4
+        for n in range(4):
+            b = lax.rem(o // group + n + 1, 4)
+            here = pl.ds(pl.multiple_of(b * some, some), some)
+            hot = turned_hots[i, here, :]
+            total = -(acc[here, :] + dot(hot, high) + dot(hot, low))
+            coded, scale = quantize(total.reshape(group, orb_dev * rows, width))
+            snd3[pl.ds(b * group, group)] = coded
+            sc_snd3[pl.ds(b * group, group)] = scale
+
+            def deliver(j, c):
+                p = b * group + j
+
+                @pl.when(p != o)
+                def _():
+                    remote(sc_snd3.at[p], sc_rec3.at[o], last, (p, f)).start()
+                    remote(snd3.at[p], rec3.at[o], last + 1, (p, f)).start()
+
+                @pl.when(p == o)
+                def _():
+                    pltpu.make_async_copy(sc_snd3.at[p], sc_rec3.at[o], recv_sem.at[last]).start()
+                    pltpu.make_async_copy(snd3.at[p], rec3.at[o], recv_sem.at[last + 1]).start()
+
+                return c
+
+            lax.fori_loop(0, group, deliver, 0)
 
     left(names, 0)
     left(held, 1)
     gone = whole.at[pl.ds(0, parts - 1)]
     pltpu.make_async_copy(gone, gone, send_sem.at[2]).wait()
-    left(sc_snd1, 3)
-    left(snd1, 4)
-    left(sc_snd2, 5)
-    left(snd2, 6)
-    left(sc_snd3, 7)
-    left(snd3, 8)
+    for i in range(chunks):
+        left(sc_snd1.at[i], 3 + i)
+        left(snd1.at[i], 3 + chunks + i)
+        left(sc_snd2.at[i], 3 + 2 * chunks + i)
+        left(snd2.at[i], 3 + 3 * chunks + i)
+    arrived(sc_rec3, last)
+    arrived(rec3, last + 1)
+    coded_ref[...] = rec3[...]
+    rate_ref[...] = sc_rec3[...]
+    left(sc_snd3, last)
+    left(snd3, last + 1)
+
+
+def unpack(rows, coded_ref, rate_ref, out_ref):
+    count, block, width = coded_ref.shape
+    for p in range(count):
+        values = restore(coded_ref[p : p + 1], rate_ref[p : p + 1])
+        out_ref[:, p * rows : (p + 1) * rows, :] = values.reshape(block // rows, rows, width)
 
 
 def tables_of(array):
@@ -402,30 +435,53 @@
     angle = angles(full_x)
     both = np.concatenate([np.cos(angle), np.sin(angle)], axis=0)
     vmem = pl.BlockSpec(memory_space=pltpu.VMEM)
-    pieces = lambda n, w, t: [pltpu.VMEM((n, block, w), t), pltpu.VMEM((n, block, w), t)]
-    rates = lambda n: [pltpu.VMEM((n, 1, LANES), F32), pltpu.VMEM((n, 1, LANES), F32)]
+    pack = 2
+    chunks = task_dev // pack
+    deep = pack * rows
+    ways = [
+        pltpu.VMEM((chunks, everyone, deep, LANES), jnp.int16), pltpu.VMEM((chunks, everyone, deep, LANES), jnp.int16),
+        pltpu.VMEM((chunks, everyone, 1, LANES), F32), pltpu.VMEM((chunks, everyone, 1, LANES), F32),
+    ]
     rows_all = task_dev * peers * rows
-    return pl.pallas_call(
+    orb_rows = peers * block
+    sems = 5 + 4 * chunks
+    coded, rate = pl.pallas_call(
         functools.partial(fused, peers, parts, rows, orb_dev, task_dev),
-        out_shape=jax.ShapeDtypeStruct((orb_dev, rows_x, width), F32),
+        out_shape=(
+            jax.ShapeDtypeStruct((peers, block, width), jnp.int16),
+            jax.ShapeDtypeStruct((peers, 1, LANES), F32),
+        ),
         in_specs=[vmem] * 6,
-        out_specs=vmem,
+        out_specs=(vmem, vmem),
         scratch_shapes=[
             pltpu.VMEM((peers, block, width), BF16),
             pltpu.VMEM((peers, task_dev, LANES), F32),
             pltpu.VMEM((parts,) + kernel.shape, F32),
             pltpu.VMEM((2, rows_all, width), BF16),
-            *pieces(everyone, LANES, jnp.int16), *rates(everyone),
-            *pieces(everyone, LANES, jnp.int16), *rates(everyone),
-            pltpu.VMEM((2, 2 * rows_all, width), BF16),
-            *pieces(peers, width, jnp.int16), *rates(peers),
-            pltpu.SemaphoreType.DMA((9,)),
-            pltpu.SemaphoreType.DMA((9,)),
+            *ways, *ways,
+            pltpu.VMEM((2, rows_all, orb_rows), BF16),
+            pltpu.VMEM((chunks, orb_rows, 2 * rows_all // chunks), BF16),
+            pltpu.VMEM((orb_rows, width), F32),
+            pltpu.VMEM((peers, block, width), jnp.int16), pltpu.VMEM((peers, block, width), jnp.int16),
+            pltpu.VMEM((peers, 1, LANES), F32), pltpu.VMEM((peers, 1, LANES), F32),
+            pltpu.SemaphoreType.DMA((sems,)),
+            pltpu.SemaphoreType.DMA((sems,)),
         ],
         compiler_params=pltpu.CompilerParams(
-            collective_id=0, has_side_effects=True, vmem_limit_bytes=60 * 1024 * 1024
+            collective_id=0, has_side_effects=True, vmem_limit_bytes=48 * 1024 * 1024
         ),
     )(sent, named, kernel[None], tables_of(forward[:, order]), tables_of(backward[order]), tables_of(both))
+    group = peers // 4
+    return pl.pallas_call(
+        functools.partial(unpack, rows),
+        grid=(4,),
+        out_shape=jax.ShapeDtypeStruct((orb_dev, rows_x, width), F32),
+        in_specs=[
+            pl.BlockSpec((group, block, width), lambda i: (i, 0, 0)),
+            pl.BlockSpec((group, 1, LANES), lambda i: (i, 0, 0)),
+        ],
+        out_specs=pl.BlockSpec((orb_dev, group * rows, width), lambda i: (0, i, 0)),
+    )(coded, rate)
 
 
 def on_device(orbitals, kernel, partner_owner, partner_local):

time: 74.6 us -> 70.3 us (0.942)
  Pallas kernels: 68.6 us -> 65 us
    pallas_call x1, Pallas kernels: 68.6 us -> 61.5 us  [fused_device(): pl.pallas_call(functools.partial(fused, peers, parts, rows, orb_dev, task...]
    pallas_call x0 -> x1, Pallas kernels: none -> 3.46 us  [fused_device(): pl.pallas_call(functools.partial(unpack, rows), grid=(4,), out_shape=jax....]
    unnamed x8 -> x19, local copies, waits for them, and re-layouts: 3.69 us -> 4.82 us
    reshape x1, local copies, waits for them, and re-layouts: 0.85 us -> 0.05 us  [fused_device(): orbitals.reshape(orb_dev, peers, rows, width).transpose(1, 0, 2, 3)]
where the time goes in v3:
time: 70.3 us; the launch traced here: 70 us
  Pallas kernels  65 us (92%)
  local copies, waits for them, and re-layouts  4.95 us (7%)
    pallas_call x1, Pallas kernels, fused_device(): pl.pallas_call(functools.partial(fused, peers, parts, rows, orb_dev, task...  61.5 us
    unnamed x19, local copies, waits for them, and re-layouts  4.82 us
    pallas_call x1, Pallas kernels, fused_device(): pl.pallas_call(functools.partial(unpack, rows), grid=(4,), out_shape=jax....  3.46 us

profile of v3, /device:TPU:13, one launch (start us, length us, event | category | flops | bytes accessed | tf_op | source)
XLA Modules:
  0.0 70.0 jit_solution(3791044180965529409)
XLA Ops:
  0.0 0.0 copy-start
  0.0 0.0 copy-start.8
  0.0 0.7 %copy-done.8 = s32[8,2,1]{0,2,1:T(1,128)S(1)} copy-done((s32[8,2,1]{0,2,1:T(1,128)S(1)}, s32[8,2,1]{0,2,1:T(1,128)}, u32[]{:S(2)}) %copy-start.8) | copy-done | bytes 88
  0.7 0.0 copy-start.7
  0.7 0.1 copy.9
  0.8 0.6 copy-done.7
  1.4 0.1 copy.10
  1.5 0.0 copy-done
  1.5 0.0 copy-start.2
  1.5 0.0 copy-start.3
  1.5 0.0 copy-start.4
  1.6 1.0 %copy-done.2 = bf16[2,512,256]{2,1,0:T(8,128)(2,1)S(1)} copy-done((bf16[2,512,256]{2,1,0:T(8,128)(2,1)S(1)}, bf16[2,512,256]{2,1,0:T(8,128)(2,1)}, u32[]{:S(2)}) %copy-start.2) | copy-done | bytes 524312
  2.6 0.1 copy-done.3
  2.6 0.1 copy-done.4
  2.7 0.0 copy-start.5
  2.7 0.9 %copy-done.5 = f32[128,256]{1,0:T(8,128)S(1)} copy-done((f32[128,256]{1,0:T(8,128)S(1)}, f32[128,256]{1,0:T(8,128)}, u32[]{:S(2)}) %copy-start.5) | copy-done | bytes 131096
  3.6 61.5 %shard_map.73 = (s16[16,64,256]{2,1,0:T(8,128)(2,1)S(1)}, f32[16,1,128]{2,1,0:T(1,128)S(1)}) custom-call(bf16[16,64,256]{2,1,0:T(8,128)(2,1)S(1)} %copy_bitcast_fusion.orb_ref, f32[8,128]{1,0:T(8,128)S(1)} %pad.4.ids_ref, f32[1,128,256]{2,1,0:T(8,128)S(1)} %bitcast.9, bf16[2,256,256]{2,1,0:T(8,128)(2,1)S(1)} %copy-done.4, ...), custom_call_target="tpu_custom_call" | custom-call | tf_op jit(solution)/shard_map/pallas_call | solution.py:448
  65.2 0.0 copy-start.1
  65.2 0.8 %copy-done.1 = s16[16,64,256]{2,1,0:T(8,128)(2,1)} copy-done((s16[16,64,256]{2,1,0:T(8,128)(2,1)}, s16[16,64,256]{2,1,0:T(8,128)(2,1)S(1)}, u32[]{:S(2)}) %copy-start.1) | copy-done | bytes 524312
  66.0 0.0 copy-start.6
  66.0 0.6 copy-done.6
  66.6 3.5 %shard_map.74 = f32[8,128,256]{2,1,0:T(8,128)} custom-call(s16[16,64,256]{2,1,0:T(8,128)(2,1)} %copy-done.1, f32[16,1,128]{2,1,0:T(1,128)} %copy-done.6), custom_call_target="tpu_custom_call" | custom-call | tf_op jit(solution)/shard_map/pallas_call | solution.py:475
  (4 shorter events, 0.1 us)
Async XLA Ops:
  0.0 1.5 %copy-start = (bf16[8,128,256]{2,1,0:T(8,128)(2,1)S(1)}, bf16[8,128,256]{2,1,0:T(8,128)(2,1)}, u32[]{:S(2)}) copy-start(bf16[8,128,256]{2,1,0:T(8,128)(2,1)} %param.7) | copy-start | bytes 1572868
  0.0 0.7 %copy-start.8 = (s32[8,2,1]{0,2,1:T(1,128)S(1)}, s32[8,2,1]{0,2,1:T(1,128)}, u32[]{:S(2)}) copy-start(s32[8,2,1]{0,2,1:T(1,128)} %param.9) | copy-start | bytes 196
  0.7 0.7 copy-start.7
  1.5 1.0 %copy-start.2 = (bf16[2,512,256]{2,1,0:T(8,128)(2,1)S(1)}, bf16[2,512,256]{2,1,0:T(8,128)(2,1)}, u32[]{:S(2)}) copy-start(bf16[2,512,256]{2,1,0:T(8,128)(2,1)} %constant.39.both_ref) | copy-start | bytes 1572868
  1.5 1.1 %copy-start.3 = (bf16[2,256,256]{2,1,0:T(8,128)(2,1)S(1)}, bf16[2,256,256]{2,1,0:T(8,128)(2,1)}, u32[]{:S(2)}) copy-start(bf16[2,256,256]{2,1,0:T(8,128)(2,1)} %constant.32.bwd_ref) | copy-start | bytes 786436
  1.5 1.2 %copy-start.4 = (bf16[2,256,256]{2,1,0:T(8,128)(2,1)S(1)}, bf16[2,256,256]{2,1,0:T(8,128)(2,1)}, u32[]{:S(2)}) copy-start(bf16[2,256,256]{2,1,0:T(8,128)(2,1)} %constant.25.fwd_ref) | copy-start | bytes 786436
  2.7 0.9 %copy-start.5 = (f32[128,256]{1,0:T(8,128)S(1)}, f32[128,256]{1,0:T(8,128)}, u32[]{:S(2)}) copy-start(f32[128,256]{1,0:T(8,128)} %param.8) | copy-start | bytes 393220
  65.2 0.8 %copy-start.1 = (s16[16,64,256]{2,1,0:T(8,128)(2,1)}, s16[16,64,256]{2,1,0:T(8,128)(2,1)S(1)}, u32[]{:S(2)}) copy-start(s16[16,64,256]{2,1,0:T(8,128)(2,1)S(1)} %get-tuple-element.7.coded_ref) | copy-start | bytes 1572868
  66.0 0.6 copy-start.6

commit v4 on v3

--- a/solution.py
+++ b/solution.py
@@ -194,9 +194,9 @@
 
 def fused(
     peers, parts, rows, orb_dev, task_dev,
-    orb_ref, ids_ref, ker_ref, fwd_ref, bwd_ref, both_ref, coded_ref, rate_ref,
-    held, names, whole, chosen, snd1, rec1, sc_snd1, sc_rec1, snd2, rec2, sc_snd2, sc_rec2,
-    hots, turned_hots, acc, snd3, rec3, sc_snd3, sc_rec3, send_sem, recv_sem,
+    orb_ref, owner_ref, local_ref, ker_ref, fwd_hbm, bwd_hbm, both_hbm, coded_ref, rate_ref,
+    ids, fwd_ref, bwd_ref, both_ref, held, names, whole, chosen, snd1, rec1, sc_snd1, sc_rec1, snd2, rec2, sc_snd2, sc_rec2,
+    hots, turned_hots, acc, snd3, rec3, sc_snd3, sc_rec3, send_sem, recv_sem, table_sem,
 ):
     o = lax.axis_index("orb")
     f = lax.axis_index("fft")
@@ -205,7 +205,7 @@
     tasks = task_dev * peers
     width = orb_ref.shape[2]
     half = width // 2
-    full_x = ker_ref.shape[2]
+    full_x = ker_ref.shape[1]
     deep = snd1.shape[2]
     chunks = snd1.shape[0]
     step = peers * deep
@@ -213,6 +213,19 @@
     norb_rows = peers * orb_dev * rows
     pack = deep // rows
 
+    fetches = [
+        pltpu.make_async_copy(src, dst, table_sem.at[n])
+        for n, (src, dst) in enumerate(((fwd_hbm, fwd_ref), (bwd_hbm, bwd_ref), (both_hbm, both_ref)))
+    ]
+    for fetch in fetches:
+        fetch.start()
+    table = jnp.zeros((task_dev, LANES), F32)
+    for t in range(task_dev):
+        for c in range(2):
+            spot = (iota(table.shape, 0) == t) & (iota(table.shape, 1) == c)
+            table = jnp.where(spot, (owner_ref[c, 0, t] * orb_dev + local_ref[c, t]).astype(F32), table)
+    ids[...] = table
+
     barrier = pltpu.get_barrier_semaphore()
 
     def greet(i, c):
@@ -229,13 +242,13 @@
             device_id=device, device_id_type=MESH,
         )
 
-    def over_orb(src, dst, k, fixed=False):
+    def over_orb(piece, dst, k):
         def one(i, c):
             p = lax.rem(o + i, peers)
-            remote(src if fixed else src.at[p], dst.at[o], k, (p, f)).start()
+            remote(piece(p), dst.at[o], k, (p, f)).start()
             return c
 
-        pltpu.make_async_copy(src if fixed else src.at[o], dst.at[o], recv_sem.at[k]).start()
+        pltpu.make_async_copy(piece(o), dst.at[o], recv_sem.at[k]).start()
         lax.fori_loop(1, peers, one, 0)
 
     def over_all(i, scale, scale_to, src, dst, k):
@@ -257,15 +270,15 @@
         gone = dst.at[pl.ds(0, dst.shape[0] - 1)]
         pltpu.make_async_copy(gone, gone, send_sem.at[k]).wait()
 
-    over_orb(ids_ref, names, 0, fixed=True)
-    over_orb(orb_ref, held, 1)
+    over_orb(lambda p: ids, names, 0)
+    over_orb(lambda p: orb_ref.at[:, pl.ds(pl.multiple_of(p * rows, rows), rows), :], held, 1)
 
     def halves(i, c):
         p = lax.rem(f + i, parts)
-        remote(ker_ref.at[0], whole.at[f], 2, (o, p)).start()
+        remote(ker_ref, whole.at[f], 2, (o, p)).start()
         return c
 
-    pltpu.make_async_copy(ker_ref.at[0], whole.at[f], recv_sem.at[2]).start()
+    pltpu.make_async_copy(ker_ref, whole.at[f], recv_sem.at[2]).start()
     lax.fori_loop(1, parts, halves, 0)
 
     def task_of(row):
@@ -303,6 +316,8 @@
     weight = jnp.concatenate([weight] * pack, axis=1)
     signed = weight * sign
 
+    for fetch in fetches:
+        fetch.wait()
     arrived(held, 1)
     source = held[...].reshape(norb_rows, width)
     for i in range(chunks):
@@ -400,11 +415,20 @@
     left(snd3, last + 1)
 
 
-def unpack(rows, coded_ref, rate_ref, out_ref):
+def unpack(rows, coded_ref, rate_ref, out_ref, done, sems):
     count, block, width = coded_ref.shape
-    for p in range(count):
-        values = restore(coded_ref[p : p + 1], rate_ref[p : p + 1])
-        out_ref[:, p * rows : (p + 1) * rows, :] = values.reshape(block // rows, rows, width)
+    group = count // 4
+    copies = []
+    for n in range(4):
+        for p in range(n * group, (n + 1) * group):
+            values = restore(coded_ref[p : p + 1], rate_ref[p : p + 1])
+            done[:, p * rows : (p + 1) * rows, :] = values.reshape(block // rows, rows, width)
+        at = slice(n * group * rows, (n + 1) * group * rows)
+        copy = pltpu.make_async_copy(done.at[:, at, :], out_ref.at[:, at, :], sems.at[n])
+        copy.start()
+        copies.append(copy)
+    for copy in copies:
+        copy.wait()
 
 
 def tables_of(array):
@@ -425,9 +449,6 @@
     half = width // 2
     per = half // parts
 
-    named = (partner_owner[:, :, 0] * orb_dev + partner_local).astype(F32)
-    named = jnp.pad(named, ((0, 0), (0, LANES - 2)))
-    sent = orbitals.reshape(orb_dev, peers, rows, width).transpose(1, 0, 2, 3).reshape(peers, block, width)
     forward, backward = packed_tables(width)
     order = np.concatenate(
         [np.concatenate([np.arange(h * per, (h + 1) * per), half + np.arange(h * per, (h + 1) * per)]) for h in range(parts)]
@@ -435,6 +456,7 @@
     angle = angles(full_x)
     both = np.concatenate([np.cos(angle), np.sin(angle)], axis=0)
     vmem = pl.BlockSpec(memory_space=pltpu.VMEM)
+    hbm = pl.BlockSpec(memory_space=pltpu.HBM)
     pack = 2
     chunks = task_dev // pack
     deep = pack * rows
@@ -451,10 +473,13 @@
             jax.ShapeDtypeStruct((peers, block, width), jnp.int16),
             jax.ShapeDtypeStruct((peers, 1, LANES), F32),
         ),
-        in_specs=[vmem] * 6,
+        in_specs=[hbm] + [pl.BlockSpec(memory_space=pltpu.SMEM)] * 2 + [hbm] * 4,
         out_specs=(vmem, vmem),
         scratch_shapes=[
-            pltpu.VMEM((peers, block, width), BF16),
+            pltpu.VMEM((task_dev, LANES), F32),
+            pltpu.VMEM((2, width, width), BF16), pltpu.VMEM((2, width, width), BF16),
+            pltpu.VMEM((2, 2 * full_x, full_x), BF16),
+            pltpu.VMEM((peers, orb_dev, rows, width), BF16),
             pltpu.VMEM((peers, task_dev, LANES), F32),
             pltpu.VMEM((parts,) + kernel.shape, F32),
             pltpu.VMEM((2, rows_all, width), BF16),
@@ -466,21 +491,22 @@
             pltpu.VMEM((peers, 1, LANES), F32), pltpu.VMEM((peers, 1, LANES), F32),
             pltpu.SemaphoreType.DMA((sems,)),
             pltpu.SemaphoreType.DMA((sems,)),
+            pltpu.SemaphoreType.DMA((3,)),
         ],
         compiler_params=pltpu.CompilerParams(
             collective_id=0, has_side_effects=True, vmem_limit_bytes=48 * 1024 * 1024
         ),
-    )(sent, named, kernel[None], tables_of(forward[:, order]), tables_of(backward[order]), tables_of(both))
-    group = peers // 4
+    )(
+        orbitals, partner_owner.transpose(1, 2, 0), partner_local.T, kernel,
+        tables_of(forward[:, order]), tables_of(backward[order]), tables_of(both),
+    )
     return pl.pallas_call(
         functools.partial(unpack, rows),
-        grid=(4,),
         out_shape=jax.ShapeDtypeStruct((orb_dev, rows_x, width), F32),
-        in_specs=[
-            pl.BlockSpec((group, block, width), lambda i: (i, 0, 0)),
-            pl.BlockSpec((group, 1, LANES), lambda i: (i, 0, 0)),
-        ],
-        out_specs=pl.BlockSpec((orb_dev, group * rows, width), lambda i: (0, i, 0)),
+        in_specs=[vmem, vmem],
+        out_specs=hbm,
+        scratch_shapes=[pltpu.VMEM((orb_dev, rows_x, width), F32), pltpu.SemaphoreType.DMA((4,))],
+        compiler_params=pltpu.CompilerParams(vmem_limit_bytes=16 * 1024 * 1024),
     )(coded, rate)
 
 

time: 70.3 us -> 69.5 us (0.989)
  Pallas kernels: 65 us -> 63.7 us
    pallas_call x1, Pallas kernels: 3.46 us -> 1.11 us  [fused_device(): pl.pallas_call(functools.partial(unpack, rows), out_shape=jax.ShapeDtypeS...]
    pallas_call x1, Pallas kernels: 61.5 us -> 62.5 us  [fused_device(): pl.pallas_call(functools.partial(fused, peers, parts, rows, orb_dev, task...]
    unnamed x19 -> x14, local copies, waits for them, and re-layouts: 4.82 us -> 5.58 us
where the time goes in v4:
time: 69.5 us; the launch traced here: 69.2 us
  Pallas kernels  63.7 us (92%)
  local copies, waits for them, and re-layouts  5.58 us (8%)
    pallas_call x1, Pallas kernels, fused_device(): pl.pallas_call(functools.partial(fused, peers, parts, rows, orb_dev, task...  62.5 us
    unnamed x14, local copies, waits for them, and re-layouts  5.58 us

profile of v4, /device:TPU:13, one launch (start us, length us, event | category | flops | bytes accessed | tf_op | source)
XLA Modules:
  0.0 69.2 jit_solution(15239408513289996156)
XLA Ops:
  0.0 0.0 copy-start.6
  0.0 0.0 copy-start.5
  0.0 0.7 copy-done.6
  0.7 0.0 copy-done.5
  0.7 0.0 copy-start
  0.7 1.0 %copy-done = bf16[8,128,256]{2,1,0:T(8,128)(2,1)S(1)} copy-done((bf16[8,128,256]{2,1,0:T(8,128)(2,1)S(1)}, bf16[8,128,256]{2,1,0:T(8,128)(2,1)}, u32[]{:S(2)}) %copy-start) | copy-done | bytes 524312
  1.7 0.0 copy-start.1
  1.7 1.0 %copy-done.1 = bf16[2,512,256]{2,1,0:T(8,128)(2,1)S(1)} copy-done((bf16[2,512,256]{2,1,0:T(8,128)(2,1)S(1)}, bf16[2,512,256]{2,1,0:T(8,128)(2,1)}, u32[]{:S(2)}) %copy-start.1) | copy-done | bytes 524312
  2.8 0.0 copy-start.2
  2.8 0.9 %copy-done.2 = bf16[2,256,256]{2,1,0:T(8,128)(2,1)S(1)} copy-done((bf16[2,256,256]{2,1,0:T(8,128)(2,1)S(1)}, bf16[2,256,256]{2,1,0:T(8,128)(2,1)}, u32[]{:S(2)}) %copy-start.2) | copy-done | bytes 262168
  3.7 0.0 copy-start.3
  3.7 0.9 %copy-done.3 = bf16[2,256,256]{2,1,0:T(8,128)(2,1)S(1)} copy-done((bf16[2,256,256]{2,1,0:T(8,128)(2,1)S(1)}, bf16[2,256,256]{2,1,0:T(8,128)(2,1)}, u32[]{:S(2)}) %copy-start.3) | copy-done | bytes 262168
  4.7 0.0 copy-start.4
  4.7 0.9 %copy-done.4 = f32[128,256]{1,0:T(8,128)S(1)} copy-done((f32[128,256]{1,0:T(8,128)S(1)}, f32[128,256]{1,0:T(8,128)}, u32[]{:S(2)}) %copy-start.4) | copy-done | bytes 131096
  5.6 62.5 %shard_map.73 = (s16[16,64,256]{2,1,0:T(8,128)(2,1)S(1)}, f32[16,1,128]{2,1,0:T(1,128)S(1)}) custom-call(bf16[8,128,256]{2,1,0:T(8,128)(2,1)S(1)} %copy-done, s32[2,1,8]{2,1,0:T(1,128)S(1)} %bitcast.2, s32[2,8]{1,0:T(2,128)S(1)} %bitcast.3, f32[128,256]{1,0:T(8,128)S(1)} %copy-done.4, bf16[2,256,256]{2,1,0:T(8,128)(2,1)S(1)} %copy-done.3, ...), custom_call_target="tpu_custom_call" | custom-call | tf_op jit(solution)/shard_map/pallas_call | solution.py:470
  68.1 1.1 %shard_map.74 = f32[8,128,256]{2,1,0:T(8,128)} custom-call(s16[16,64,256]{2,1,0:T(8,128)(2,1)S(1)} %get-tuple-element.7.coded_ref, f32[16,1,128]{2,1,0:T(1,128)S(1)} %get-tuple-element.8.rate_ref), custom_call_target="tpu_custom_call" | custom-call | tf_op jit(solution)/shard_map/pallas_call | solution.py:503
Async XLA Ops:
  0.0 0.7 copy-start.6
  0.0 0.7 %copy-start.5 = (s32[8,2,1]{0,2,1:T(1,128)S(1)}, s32[8,2,1]{0,2,1:T(1,128)}, u32[]{:S(2)}) copy-start(s32[8,2,1]{0,2,1:T(1,128)} %param.9) | copy-start | bytes 196
  0.7 1.0 %copy-start = (bf16[8,128,256]{2,1,0:T(8,128)(2,1)S(1)}, bf16[8,128,256]{2,1,0:T(8,128)(2,1)}, u32[]{:S(2)}) copy-start(bf16[8,128,256]{2,1,0:T(8,128)(2,1)} %orb_ref.1) | copy-start | bytes 1572868
  1.7 1.0 %copy-start.1 = (bf16[2,512,256]{2,1,0:T(8,128)(2,1)S(1)}, bf16[2,512,256]{2,1,0:T(8,128)(2,1)}, u32[]{:S(2)}) copy-start(bf16[2,512,256]{2,1,0:T(8,128)(2,1)} %constant.32.both_hbm) | copy-start | bytes 1572868
  2.8 0.9 %copy-start.2 = (bf16[2,256,256]{2,1,0:T(8,128)(2,1)S(1)}, bf16[2,256,256]{2,1,0:T(8,128)(2,1)}, u32[]{:S(2)}) copy-start(bf16[2,256,256]{2,1,0:T(8,128)(2,1)} %constant.25.bwd_hbm) | copy-start | bytes 786436
  3.7 0.9 %copy-start.3 = (bf16[2,256,256]{2,1,0:T(8,128)(2,1)S(1)}, bf16[2,256,256]{2,1,0:T(8,128)(2,1)}, u32[]{:S(2)}) copy-start(bf16[2,256,256]{2,1,0:T(8,128)(2,1)} %constant.18.fwd_hbm) | copy-start | bytes 786436
  4.7 0.9 %copy-start.4 = (f32[128,256]{1,0:T(8,128)S(1)}, f32[128,256]{1,0:T(8,128)}, u32[]{:S(2)}) copy-start(f32[128,256]{1,0:T(8,128)} %ker_ref.1) | copy-start | bytes 393220

commit v5 on v4

--- a/solution.py
+++ b/solution.py
@@ -12,6 +12,7 @@
 LEVELS = 32767.0
 STEPS = 128.0
 LANES = 128
+VMEM_GRANT = 66469888
 
 
 def angles(length):
@@ -415,11 +416,19 @@
     left(snd3, last + 1)
 
 
-def unpack(rows, coded_ref, rate_ref, out_ref, done, sems):
+def unpack(rows, coded_hbm, rate_hbm, out_ref, coded_ref, rate_ref, done, sems):
     count, block, width = coded_ref.shape
     group = count // 4
+    fetches = [pltpu.make_async_copy(rate_hbm, rate_ref, sems.at[4])]
+    for n in range(4):
+        at = pl.ds(n * group, group)
+        fetches.append(pltpu.make_async_copy(coded_hbm.at[at], coded_ref.at[at], sems.at[5 + n]))
+    for fetch in fetches:
+        fetch.start()
+    fetches[0].wait()
     copies = []
     for n in range(4):
+        fetches[1 + n].wait()
         for p in range(n * group, (n + 1) * group):
             values = restore(coded_ref[p : p + 1], rate_ref[p : p + 1])
             done[:, p * rows : (p + 1) * rows, :] = values.reshape(block // rows, rows, width)
@@ -494,7 +503,7 @@
             pltpu.SemaphoreType.DMA((3,)),
         ],
         compiler_params=pltpu.CompilerParams(
-            collective_id=0, has_side_effects=True, vmem_limit_bytes=48 * 1024 * 1024
+            collective_id=0, has_side_effects=True, vmem_limit_bytes=VMEM_GRANT
         ),
     )(
         orbitals, partner_owner.transpose(1, 2, 0), partner_local.T, kernel,
@@ -503,10 +512,13 @@
     return pl.pallas_call(
         functools.partial(unpack, rows),
         out_shape=jax.ShapeDtypeStruct((orb_dev, rows_x, width), F32),
-        in_specs=[vmem, vmem],
+        in_specs=[hbm, hbm],
         out_specs=hbm,
-        scratch_shapes=[pltpu.VMEM((orb_dev, rows_x, width), F32), pltpu.SemaphoreType.DMA((4,))],
-        compiler_params=pltpu.CompilerParams(vmem_limit_bytes=16 * 1024 * 1024),
+        scratch_shapes=[
+            pltpu.VMEM((peers, block, width), jnp.int16), pltpu.VMEM((peers, 1, LANES), F32),
+            pltpu.VMEM((orb_dev, rows_x, width), F32), pltpu.SemaphoreType.DMA((9,)),
+        ],
+        compiler_params=pltpu.CompilerParams(vmem_limit_bytes=VMEM_GRANT),
     )(coded, rate)
 
 

time: 69.5 us -> 65.8 us (0.947)
  local copies, waits for them, and re-layouts: 5.58 us -> 0 us
  Pallas kernels: 63.7 us -> 65.6 us
    unnamed x14 -> x0, local copies, waits for them, and re-layouts: 5.58 us -> none
    pallas_call x1, Pallas kernels: 1.11 us -> 2.15 us  [fused_device(): pl.pallas_call(functools.partial(unpack, rows), out_shape=jax.ShapeDtypeS...]
    pallas_call x1, Pallas kernels: 62.5 us -> 63.4 us  [fused_device(): pl.pallas_call(functools.partial(fused, peers, parts, rows, orb_dev, task...]
where the time goes in v5:
time: 65.8 us; the launch traced here: 65.6 us
  Pallas kernels  65.6 us (100%)
    pallas_call x1, Pallas kernels, fused_device(): pl.pallas_call(functools.partial(fused, peers, parts, rows, orb_dev, task...  63.4 us
    pallas_call x1, Pallas kernels, fused_device(): pl.pallas_call(functools.partial(unpack, rows), out_shape=jax.ShapeDtypeS...  2.15 us

profile of v5, /device:TPU:13, one launch (start us, length us, event | category | flops | bytes accessed | tf_op | source)
XLA Modules:
  0.0 65.6 jit_solution(7323379313412017084)
XLA Ops:
  0.0 63.4 %shard_map.73 = (s16[16,64,256]{2,1,0:T(8,128)(2,1)}, f32[16,1,128]{2,1,0:T(1,128)}) custom-call(bf16[8,128,256]{2,1,0:T(8,128)(2,1)} %orb_ref.1, s32[2,1,8]{2,1,0:T(1,128)} %bitcast.2, s32[2,8]{1,0:T(2,128)} %bitcast.3, f32[128,256]{1,0:T(8,128)} %ker_ref.1, bf16[2,256,256]{2,1,0:T(8,128)(2,1)} %constant.18.fwd_hbm, bf16[2,256,256]{2,1,0:T(8,128)(2,1)} %constant.25.bwd_hbm, ...), custom_call_target="tpu_custom_call" | custom-call | tf_op jit(solution)/shard_map/pallas_call | solution.py:479
  63.4 2.1 %shard_map.74 = f32[8,128,256]{2,1,0:T(8,128)} custom-call(s16[16,64,256]{2,1,0:T(8,128)(2,1)} %get-tuple-element.7.coded_hbm, f32[16,1,128]{2,1,0:T(1,128)} %get-tuple-element.8.rate_hbm), custom_call_target="tpu_custom_call" | custom-call | tf_op jit(solution)/shard_map/pallas_call | solution.py:512

commit v6 on v5

--- a/solution.py
+++ b/solution.py
@@ -203,6 +203,7 @@
     f = lax.axis_index("fft")
     everyone = peers * parts
     me = f * peers + o
+    turn = jnp.where(2 * o < peers, peers - 1, 1)
     tasks = task_dev * peers
     width = orb_ref.shape[2]
     half = width // 2
@@ -245,7 +246,7 @@
 
     def over_orb(piece, dst, k):
         def one(i, c):
-            p = lax.rem(o + i, peers)
+            p = lax.rem(o + turn * i, peers)
             remote(piece(p), dst.at[o], k, (p, f)).start()
             return c
 
@@ -254,8 +255,8 @@
 
     def over_all(i, scale, scale_to, src, dst, k):
         def one(j, c):
-            p = lax.rem(me + j, everyone)
-            device = (lax.rem(p, peers), p // peers)
+            device = (lax.rem(o + turn * (j // parts), peers), lax.rem(f + j, parts))
+            p = device[1] * peers + device[0]
             remote(scale.at[i, p], scale_to.at[i, me], k + i, device).start()
             remote(src.at[i, p], dst.at[i, me], k + chunks + i, device).start()
             return c

time: 65.8 us -> 66.3 us (level)
  no operation moved by 1% of the time
where the time goes in v6:
time: 66.3 us; the launch traced here: 65.9 us
  Pallas kernels  65.9 us (99%)
    pallas_call x1, Pallas kernels, fused_device(): pl.pallas_call(functools.partial(fused, peers, parts, rows, orb_dev, task...  63.8 us
    pallas_call x1, Pallas kernels, fused_device(): pl.pallas_call(functools.partial(unpack, rows), out_shape=jax.ShapeDtypeS...  2.15 us

profile of v6, /device:TPU:13, one launch (start us, length us, event | category | flops | bytes accessed | tf_op | source)
XLA Modules:
  0.0 65.9 jit_solution(17701570226984521898)
XLA Ops:
  0.0 63.8 %shard_map.73 = (s16[16,64,256]{2,1,0:T(8,128)(2,1)}, f32[16,1,128]{2,1,0:T(1,128)}) custom-call(bf16[8,128,256]{2,1,0:T(8,128)(2,1)} %orb_ref.1, s32[2,1,8]{2,1,0:T(1,128)} %bitcast.2, s32[2,8]{1,0:T(2,128)} %bitcast.3, f32[128,256]{1,0:T(8,128)} %ker_ref.1, bf16[2,256,256]{2,1,0:T(8,128)(2,1)} %constant.18.fwd_hbm, bf16[2,256,256]{2,1,0:T(8,128)(2,1)} %constant.25.bwd_hbm, ...), custom_call_target="tpu_custom_call" | custom-call | tf_op jit(solution)/shard_map/pallas_call | solution.py:480
  63.8 2.1 %shard_map.74 = f32[8,128,256]{2,1,0:T(8,128)} custom-call(s16[16,64,256]{2,1,0:T(8,128)(2,1)} %get-tuple-element.7.coded_hbm, f32[16,1,128]{2,1,0:T(1,128)} %get-tuple-element.8.rate_hbm), custom_call_target="tpu_custom_call" | custom-call | tf_op jit(solution)/shard_map/pallas_call | solution.py:513
